TPU v7x, 256 devices: a whole 4x4x8 slice. The times are simulated.
256 devices in a mesh: segment: 2 (over core), dp: 16 (over y_lo, z), tensor: 8 (over x, y_hi).
Axes of the slice: x: 4, y: 4 (y_hi: 2, y_lo: 2; y = y_hi * 2 + y_lo), z: 8, core: 2. Of those that a mesh axis runs over, the one named last changes fastest.
Arguments:
- tokens: bfloat16 [256, 5120], P('dp'), may hold values from -12 to 12
- cotangent: bfloat16 [256, 5120], P('dp'), may hold values from -6 to 6
- gains: float32 [2, 5120], P('segment'), may hold values from 0.1 to 1.9
- w_gate: bfloat16 [2, 5120, 27648], P('segment', 'dp', 'tensor'), may hold values from -0.078125 to 0.078125
- w_up: bfloat16 [2, 5120, 27648], P('segment', 'dp', 'tensor'), may hold values from -0.078125 to 0.078125
- w_down: bfloat16 [2, 5120, 27648], P('segment', 'dp', 'tensor'), may hold values from -0.0390625 to 0.0390625
Outputs:
- acts: bfloat16 [2, 256, 5120], P('segment', 'dp')
- grads: bfloat16 [2, 256, 5120], P('segment', 'dp')
All inputs are finite; a program needn't handle non-finite values.
Results may differ from a plain program's by a relative error of at most 0.04.
Values may be sent and summed in bfloat16 or wider, within the bound.
A program may use at most 64 MiB of HBM per device.

v0:
```python
import jax
import jax.numpy as jnp
from jax import lax
from jax.sharding import PartitionSpec as P

EPSILON = 1e-06


def sent_together(arrays, axis, dim, along):
    ends, at = ([], 0)
    for a in arrays[:-1]:
        at += a.shape[along]
        ends.append(at)
    both = jnp.concatenate(arrays, axis=along)
    return tuple(
        jnp.split(lax.psum_scatter(both, axis, scatter_dimension=dim, tiled=True), ends, axis=along)
    )


def copy_for_each(x, axis):
    copies = jnp.broadcast_to(x, (lax.axis_size(axis), *x.shape))
    return lax.all_to_all(copies, axis, split_axis=0, concat_axis=0, tiled=True)


def taken_together(x, axis):
    return copy_for_each(x, axis).astype(jnp.float32).sum(axis=0)


def in_order(blocks, dim):
    blocks = jnp.moveaxis(blocks, 0, dim)
    lengths = blocks.shape
    return blocks.reshape(*lengths[:dim], lengths[dim] * lengths[dim + 1], *lengths[dim + 2 :])


def gathered_copies(x, axis, dim):
    blocks = copy_for_each(x, axis)
    return in_order(blocks, dim)


def turned_gather(arrays, axis, dims):
    turned = [jnp.moveaxis(a, dim, 0) for a, dim in zip(arrays, dims)]
    both = jnp.concatenate([t.reshape(len(t), -1) for t in turned], axis=1)
    out, at, done = (lax.all_gather(both, axis, axis=0, tiled=True), 0, [])
    for t, dim in zip(turned, dims):
        slab = out[:, at : at + t[0].size].reshape(-1, *t.shape[1:])
        done.append(jnp.moveaxis(slab, 0, dim))
        at += t[0].size
    return tuple(done)


def from_behind(value, axis, steps):
    count = lax.axis_size(axis)
    leading, last = (max(0, -steps), min(count, count - steps))
    return lax.ppermute(value, axis, [(source, source + steps) for source in range(leading, last)])


def split_up(x, dim, length):
    lengths = x.shape
    blocks = x.reshape(*lengths[:dim], length, lengths[dim] // length, *lengths[dim + 1 :])
    return jnp.moveaxis(blocks, dim, 0)


def sent_and_summed(x, axis, dim):
    blocks = split_up(x, dim, lax.axis_size(axis))
    arrived = lax.all_to_all(blocks, axis, split_axis=0, concat_axis=0, tiled=True)
    return arrived.astype(jnp.float32).sum(axis=0)


def normalize(values):
    wide = values.astype(jnp.float32)
    inverse = lax.rsqrt(jnp.mean(wide * wide, axis=1, keepdims=True) + EPSILON)
    return (wide, wide * inverse, inverse)


def contract_last(left, right):
    return lax.dot_general(
        left, right, (((1,), (1,)), ((), ())), preferred_element_type=jnp.float32
    )


def input_grads(d_hidden, stash_gate, stash_up):
    gate_pre = stash_gate.astype(jnp.float32)
    up_pre = stash_up.astype(jnp.float32)
    sigmoid_gate = jax.nn.sigmoid(gate_pre)
    d_gate = (d_hidden * up_pre * sigmoid_gate * (1.0 + gate_pre * (1.0 - sigmoid_gate))).astype(
        jnp.bfloat16
    )
    d_up = (d_hidden * gate_pre * sigmoid_gate).astype(jnp.bfloat16)
    return (d_gate, d_up)


def norm_back(unit, inverse, gain_row, d_normed, incoming):
    weighted = d_normed * gain_row
    projection = jnp.mean(weighted * unit, axis=1, keepdims=True)
    return (incoming.astype(jnp.float32) + inverse * (weighted - unit * projection)).astype(
        jnp.bfloat16
    )


def unchanged(current):
    return current


def to_columns(rows_here):
    return lax.all_to_all(rows_here, "dp", split_axis=1, concat_axis=0, tiled=True)


def hidden_sums(first_term, second_term):
    return tuple(
        (
            part.astype(jnp.float32)
            for part in sent_together(
                (first_term.astype(jnp.bfloat16), second_term.astype(jnp.bfloat16)), "dp", 1, 0
            )
        )
    )


def sum_back(partial_value, complete):
    own_rows = partial_value.shape[0] // lax.axis_size("dp")
    summed = taken_together(partial_value.astype(jnp.bfloat16), "tensor").astype(jnp.float32)
    rows_values = lax.all_to_all(
        summed.astype(jnp.bfloat16), "dp", split_axis=0, concat_axis=1, tiled=True
    ).astype(summed.dtype)
    return complete(rows_values, 0, own_rows)


def body(tokens, cotangent, gains, w_gate, w_up, w_down):
    gate_weight = w_gate[0]
    up_weight = w_up[0]
    down_weight = w_down[0]
    column_block = gate_weight.shape[0]
    hidden_block = gate_weight.shape[1]
    leading = lax.axis_index("segment") == 0
    trailing = jnp.logical_not(leading)

    def output_rows(wide):

        def complete(values, first_row, count):
            return (wide + values).astype(jnp.bfloat16)

        return complete

    def gradient_rows(unit, inverse, incoming):

        def complete(values, first_row, count):
            return norm_back(unit, inverse, gains, values, incoming)

        return complete

    def fold_down(hidden, active):
        initial = jnp.zeros((hidden.shape[0], column_block), jnp.float32)
        piece = gathered_copies(hidden, "dp", 1)

        def compute(current):
            return contract_last(piece, down_weight)

        return lax.cond(active, compute, unchanged, initial)

    def fold_back(d_gate, d_up, active):
        initial = jnp.zeros((d_gate.shape[0], column_block), jnp.float32)
        pieces = turned_gather((d_gate, d_up), "dp", (1, 1))

        def compute(current):
            return contract_last(pieces[0], gate_weight) + contract_last(pieces[1], up_weight)

        return lax.cond(active, compute, unchanged, initial)

    def forward_terms(columns):
        return (
            jnp.dot(columns, gate_weight, preferred_element_type=jnp.float32),
            jnp.dot(columns, up_weight, preferred_element_type=jnp.float32),
        )

    def late_grad_terms(columns):
        return (
            jnp.dot(columns, down_weight, preferred_element_type=jnp.float32),
            jnp.zeros((columns.shape[0], hidden_block), jnp.float32),
        )

    def spare_terms(columns):
        empty = jnp.zeros((columns.shape[0], hidden_block), jnp.float32)
        return (empty, empty)

    wide_in, unit_in, inverse_in = normalize(tokens)
    normed_in = (unit_in * gains).astype(jnp.bfloat16)
    entry_cols = to_columns(jnp.where(leading, normed_in, cotangent))
    first_part, second_part = lax.cond(leading, forward_terms, late_grad_terms, entry_cols)
    first_sum, second_sum = hidden_sums(first_part, second_part)
    early_gate = first_sum.astype(jnp.bfloat16)
    early_up = second_sum.astype(jnp.bfloat16)
    early_hidden = (jax.nn.silu(first_sum) * second_sum).astype(jnp.bfloat16)
    early_out = sum_back(fold_down(early_hidden, leading), output_rows(wide_in))
    arrived = from_behind(early_out, "segment", 1)
    wide_mid, unit_mid, inverse_mid = normalize(arrived)
    normed_mid = (unit_mid * gains).astype(jnp.bfloat16)
    mid_cols = to_columns(normed_mid)
    gate_part, up_part = lax.cond(leading, spare_terms, forward_terms, mid_cols)
    late_gate_sum, late_up_sum = hidden_sums(gate_part, up_part)
    late_gate = late_gate_sum.astype(jnp.bfloat16)
    late_up = late_up_sum.astype(jnp.bfloat16)
    late_hidden = (jax.nn.silu(late_gate_sum) * late_up_sum).astype(jnp.bfloat16)
    late_d_gate, late_d_up = input_grads(first_sum, late_gate, late_up)
    late_out = sum_back(fold_down(late_hidden, trailing), output_rows(wide_mid))
    d_mid = sum_back(
        fold_back(late_d_gate, late_d_up, trailing), gradient_rows(unit_mid, inverse_mid, cotangent)
    )
    returned = from_behind(d_mid, "segment", -1)
    kept_gate, kept_up = (early_gate, early_up)
    back_cols = to_columns(returned)

    def early_grad_term(columns):
        return jnp.dot(columns, down_weight, preferred_element_type=jnp.float32)

    def spare_term(columns):
        return jnp.zeros((columns.shape[0], hidden_block), jnp.float32)

    grad_part = lax.cond(leading, early_grad_term, spare_term, back_cols)
    d_hidden_early = sent_and_summed(grad_part.astype(jnp.bfloat16), "dp", 1)
    early_d_gate, early_d_up = input_grads(d_hidden_early, kept_gate, kept_up)
    d_tokens = sum_back(
        fold_back(early_d_gate, early_d_up, leading), gradient_rows(unit_in, inverse_in, returned)
    )
    acts = jnp.where(leading, early_out, late_out)[None]
    grads = jnp.where(leading, d_tokens, d_mid)[None]
    return (acts, grads)


def solution(mesh):
    in_specs = (
        P("dp", None),
        P("dp", None),
        P("segment", None),
        P("segment", "dp", "tensor"),
        P("segment", "dp", "tensor"),
        P("segment", "dp", "tensor"),
    )
    out_specs = (P("segment", "dp", None), P("segment", "dp", None))
    return jax.shard_map(body, mesh=mesh, in_specs=in_specs, out_specs=out_specs, check_vma=False)
```

profile of v0, /device:TPU:8, one launch (start us, length us, event | category | flops | bytes accessed | tf_op | source)
XLA Modules:
  0.0 638.3 jit_solution(6151462651268929296)
XLA Ops:
  10.2 9.9 %all-to-all-start = ((bf16[16,16,320]{2,0,1:T(8,128)(2,1)}), bf16[16,16,320]{2,0,1:T(8,128)(2,1)S(1)}, u32[]{:S(2)}, u32[]{:S(2)}) async-start(bf16[16,16,320]{2,0,1:T(8,128)(2,1)} %copy.55), calls=%async_computation | async-start | bytes 393216 | tf_op jit(solution)/shard_map/all_to_all | solution.py:105
  20.2 8.4 %all-to-all-done = bf16[16,16,320]{2,0,1:T(8,128)(2,1)S(1)} async-done(((bf16[16,16,320]{2,0,1:T(8,128)(2,1)}), bf16[16,16,320]{2,0,1:T(8,128)(2,1)S(1)}, u32[]{:S(2)}, u32[]{:S(2)}) %all-to-all-start) | async-done | bytes 163872 | tf_op jit(solution)/shard_map/all_to_all | solution.py:105
  28.6 4.9 conditional.7
  37.6 3.6 copy.79
  41.2 77.3 %reduce-scatter.7.cloned.1.call-done = bf16[216,512]{1,0:T(8,128)(2,1)} async-done(((bf16[3456,512]{1,0:T(8,128)(2,1)}), bf16[216,512]{1,0:T(8,128)(2,1)}) %reduce-scatter.7.cloned.1.call-update) | async-done | bytes 221200
  120.8 5.7 all-to-all-start.1
  126.5 32.1 %all-to-all-done.1 = bf16[16,256,216]{1,2,0:T(8,128)(2,1)} async-done(((bf16[16,256,216]{1,2,0:T(8,128)(2,1)}), bf16[16,256,216]{1,2,0:T(8,128)(2,1)}, u32[]{:S(2)}, u32[]{:S(2)}) %all-to-all-start.1) | async-done | bytes 1769504 | tf_op jit(solution)/shard_map/all_to_all | solution.py:22
  160.9 20.3 %all_to_all.144 = bf16[8,256,320]{1,2,0:T(8,128)(2,1)S(1)} all-to-all(bf16[8,256,320]{1,2,0:T(8,128)(2,1)S(1)} %broadcast_in_dim.29), channel_id=1, replica_groups=mesh['segment'=2,'dp'=16,'tensor'=8] {'tensor'}, dimensions={0} | all-to-all | bytes 2621440 | tf_op jit(solution)/shard_map/all_to_all | solution.py:22
  181.6 13.0 %all_to_all.145 = bf16[16,16,320]{2,1,0:T(8,128)(2,1)S(1)} all-to-all(bf16[16,16,320]{2,1,0:T(8,128)(2,1)S(1)} %bitcast.103), channel_id=1, replica_groups=mesh['segment'=2,'dp'=16,'tensor'=8] {'dp'}, dimensions={0} | all-to-all | bytes 327680 | tf_op jit(solution)/shard_map/all_to_all | solution.py:122
  199.2 4.8 all-to-all-start.4
  204.0 8.7 %all-to-all-done.4 = bf16[16,16,320]{2,0,1:T(8,128)(2,1)S(1)} async-done(((bf16[16,16,320]{2,0,1:T(8,128)(2,1)}), bf16[16,16,320]{2,0,1:T(8,128)(2,1)S(1)}, u32[]{:S(2)}, u32[]{:S(2)}) %all-to-all-start.4) | async-done | bytes 163872 | tf_op jit(solution)/shard_map/all_to_all | solution.py:105
  216.9 3.6 copy.81
  220.6 75.9 %reduce-scatter.9.cloned.1.call-done = bf16[216,512]{1,0:T(8,128)(2,1)} async-done(((bf16[3456,512]{1,0:T(8,128)(2,1)}), bf16[216,512]{1,0:T(8,128)(2,1)}) %reduce-scatter.9.cloned.1.call-update) | async-done | bytes 221200
  299.0 71.3 %all-gather.3.cloned.1.call-done = bf16[3456,512]{1,0:T(8,128)(2,1)} async-done(((bf16[216,512]{1,0:T(8,128)(2,1)}), bf16[3456,512]{1,0:T(8,128)(2,1)}) %all-gather.3.cloned.1.call-update) | async-done | bytes 3538960 | tf_op jit(solution)/shard_map/all_gather | solution.py:43
  370.3 4.0 slice_bitcast_fusion.2
  374.6 19.9 %all_to_all.146 = bf16[8,256,320]{1,2,0:T(8,128)(2,1)S(1)} all-to-all(bf16[8,256,320]{1,2,0:T(8,128)(2,1)S(1)} %broadcast_in_dim.33), channel_id=1, replica_groups=mesh['segment'=2,'dp'=16,'tensor'=8] {'tensor'}, dimensions={0} | all-to-all | bytes 2621440 | tf_op jit(solution)/shard_map/all_to_all | solution.py:22
  395.0 12.8 %all_to_all.147 = bf16[16,16,320]{2,1,0:T(8,128)(2,1)S(1)} all-to-all(bf16[16,16,320]{2,1,0:T(8,128)(2,1)S(1)} %bitcast.104), channel_id=1, replica_groups=mesh['segment'=2,'dp'=16,'tensor'=8] {'dp'}, dimensions={0} | all-to-all | bytes 327680 | tf_op jit(solution)/shard_map/all_to_all | solution.py:122
  412.9 4.8 all-to-all-start.10
  417.7 8.5 %all-to-all-done.10 = bf16[16,16,320]{2,0,1:T(8,128)(2,1)S(1)} async-done(((bf16[16,16,320]{2,0,1:T(8,128)(2,1)}), bf16[16,16,320]{2,0,1:T(8,128)(2,1)S(1)}, u32[]{:S(2)}, u32[]{:S(2)}) %all-to-all-start.10) | async-done | bytes 163872 | tf_op jit(solution)/shard_map/all_to_all | solution.py:105
  428.5 3.9 copy.70
  432.4 46.0 %all_to_all.148 = bf16[16,256,216]{1,2,0:T(8,128)(2,1)S(1)} all-to-all(bf16[16,256,216]{1,2,0:T(8,128)(2,1)} %bitcast.92), channel_id=1, replica_groups=mesh['segment'=2,'dp'=16,'tensor'=8] {'dp'}, dimensions={0} | all-to-all | bytes 3538944 | tf_op jit(solution)/shard_map/all_to_all | solution.py:65
  480.9 4.9 all-to-all-start.5
  485.8 55.7 %all-to-all-done.5 = bf16[16,256,216]{1,2,0:T(8,128)(2,1)} async-done(((bf16[16,256,216]{1,2,0:T(8,128)(2,1)}), bf16[16,256,216]{1,2,0:T(8,128)(2,1)}, u32[]{:S(2)}, u32[]{:S(2)}) %all-to-all-start.5) | async-done | bytes 1769504 | tf_op jit(solution)/shard_map/all_to_all | solution.py:22
  542.6 3.6 all-to-all-start.6
  546.2 30.6 %all-to-all-done.6 = bf16[8,256,320]{1,2,0:T(8,128)(2,1)S(1)} async-done(((bf16[8,256,320]{1,2,0:T(8,128)(2,1)}), bf16[8,256,320]{1,2,0:T(8,128)(2,1)S(1)}, u32[]{:S(2)}, u32[]{:S(2)}) %all-to-all-start.6) | async-done | bytes 1310752 | tf_op jit(solution)/shard_map/all_to_all | solution.py:22
  577.8 4.7 all-to-all-start.7
  582.5 4.2 slice_bitcast_fusion
  586.7 3.4 conditional.13
  592.1 5.1 all-to-all-start.12
  597.5 16.8 %all-to-all-done.12 = bf16[8,256,320]{1,2,0:T(8,128)(2,1)S(1)} async-done(((bf16[8,256,320]{1,2,0:T(8,128)(2,1)}), bf16[8,256,320]{1,2,0:T(8,128)(2,1)S(1)}, u32[]{:S(2)}, u32[]{:S(2)}) %all-to-all-start.12) | async-done | bytes 1310752 | tf_op jit(solution)/shard_map/all_to_all | solution.py:22
  615.3 7.1 %all-to-all-start.13 = ((bf16[16,16,320]{2,1,0:T(8,128)(2,1)}), bf16[16,16,320]{2,1,0:T(8,128)(2,1)S(1)}, u32[]{:S(2)}, u32[]{:S(2)}) async-start(bf16[16,16,320]{2,1,0:T(8,128)(2,1)} %bitcast.32), calls=%async_computation.13 | async-start | bytes 393216 | tf_op jit(solution)/shard_map/all_to_all | solution.py:122
  623.1 7.2 %all-to-all-done.13 = bf16[16,16,320]{2,1,0:T(8,128)(2,1)S(1)} async-done(((bf16[16,16,320]{2,1,0:T(8,128)(2,1)}), bf16[16,16,320]{2,1,0:T(8,128)(2,1)S(1)}, u32[]{:S(2)}, u32[]{:S(2)}) %all-to-all-start.13) | async-done | bytes 163872 | tf_op jit(solution)/shard_map/all_to_all | solution.py:122
  (131 shorter events, 54.4 us)
Async XLA Ops:
  10.2 18.4 %all-to-all-start = ((bf16[16,16,320]{2,0,1:T(8,128)(2,1)}), bf16[16,16,320]{2,0,1:T(8,128)(2,1)S(1)}, u32[]{:S(2)}, u32[]{:S(2)}) async-start(bf16[16,16,320]{2,0,1:T(8,128)(2,1)} %copy.55), calls=%async_computation | async-start | bytes 393216 | tf_op jit(solution)/shard_map/all_to_all | solution.py:105
  20.1 98.3 %reduce-scatter.7.cloned.1.call-start = ((), (), s32[]{:S(2)}) async-start(), calls=%async_computation.18 | async-start | bytes 3760128
  28.6 2.9 copy-start.17
  28.6 2.9 copy-start.5
  120.8 37.8 %copy-start = (bf16[1,320,3456]{2,1,0:T(8,128)(2,1)S(1)}, bf16[1,320,3456]{2,1,0:T(8,128)(2,1)}, u32[]{:S(2)}) copy-start(bf16[1,320,3456]{2,1,0:T(8,128)(2,1)} %param.25) | copy-start | bytes 6635524
  120.8 37.8 %all-to-all-start.1 = ((bf16[16,256,216]{1,2,0:T(8,128)(2,1)}), bf16[16,256,216]{1,2,0:T(8,128)(2,1)}, u32[]{:S(2)}, u32[]{:S(2)}) async-start(bf16[16,256,216]{1,2,0:T(8,128)(2,1)} %broadcast_in_dim.28), calls=%async_computation.1 | async-start | bytes 3538944 | tf_op jit(solution)/shard_map/all_to_all | solution.py:22
  181.4 13.6 %copy-start.13 = (bf16[16,5120]{1,0:T(8,128)(2,1)S(1)}, bf16[16,5120]{1,0:T(8,128)(2,1)}, u32[]{:S(2)}) copy-start(bf16[16,5120]{1,0:T(8,128)(2,1)} %param.20) | copy-start | bytes 491524
  181.5 16.7 %copy-start.21 = (f32[1,5120]{1,0:T(1,128)S(1)}, f32[1,5120]{1,0:T(1,128)}, u32[]{:S(2)}) copy-start(f32[1,5120]{1,0:T(1,128)} %param.22) | copy-start | bytes 61444
  194.7 17.9 %copy-start.2 = (bf16[1,320,3456]{2,1,0:T(8,128)(2,1)S(1)}, bf16[1,320,3456]{2,1,0:T(8,128)(2,1)}, u32[]{:S(2)}) copy-start(bf16[1,320,3456]{2,1,0:T(8,128)(2,1)} %param.23) | copy-start | bytes 6635524
  195.1 2.6 copy-start.24
  195.1 2.4 collective-permute-start
  199.2 13.5 %all-to-all-start.4 = ((bf16[16,16,320]{2,0,1:T(8,128)(2,1)}), bf16[16,16,320]{2,0,1:T(8,128)(2,1)S(1)}, u32[]{:S(2)}, u32[]{:S(2)}) async-start(bf16[16,16,320]{2,0,1:T(8,128)(2,1)} %copy.60), calls=%async_computation.4 | async-start | bytes 393216 | tf_op jit(solution)/shard_map/all_to_all | solution.py:105
  203.9 92.5 %reduce-scatter.9.cloned.1.call-start = ((), (), s32[]{:S(2)}) async-start(), calls=%async_computation.19 | async-start | bytes 3760128
  220.5 75.9 %copy-start.20 = (bf16[216,512]{1,0:T(8,128)(2,1)S(1)}, bf16[216,512]{1,0:T(8,128)(2,1)}, u32[]{:S(2)}) copy-start(bf16[216,512]{1,0:T(8,128)(2,1)} %reduce-scatter.7.cloned.1.call-done) | copy-start | bytes 663556
  220.6 149.7 %all-gather.3.cloned.1.call-start = ((), (), s32[]{:S(2)}) async-start(), calls=%async_computation.16 | async-start | bytes 3760128 | tf_op jit(solution)/shard_map/all_gather | solution.py:43
  298.9 75.4 %copy-start.3 = (bf16[1,320,3456]{2,1,0:T(8,128)(2,1)S(1)}, bf16[1,320,3456]{2,1,0:T(8,128)(2,1)}, u32[]{:S(2)}) copy-start(bf16[1,320,3456]{2,1,0:T(8,128)(2,1)} %param.23) | copy-start | bytes 6635524
  394.8 13.4 %copy-start.16 = (bf16[16,5120]{1,0:T(8,128)(2,1)S(1)}, bf16[16,5120]{1,0:T(8,128)(2,1)}, u32[]{:S(2)}) copy-start(bf16[16,5120]{1,0:T(8,128)(2,1)} %copy-done.15) | copy-start | bytes 491524
  394.8 13.4 %copy-start.22 = (f32[1,5120]{1,0:T(1,128)S(1)}, f32[1,5120]{1,0:T(1,128)}, u32[]{:S(2)}) copy-start(f32[1,5120]{1,0:T(1,128)} %param.22) | copy-start | bytes 61444
  394.8 13.6 %copy-start.23 = (bf16[16,5120]{1,0:T(8,128)(2,1)S(1)}, bf16[16,5120]{1,0:T(8,128)(2,1)}, u32[]{:S(2)}) copy-start(bf16[16,5120]{1,0:T(8,128)(2,1)} %param.21) | copy-start | bytes 491524
  408.0 18.2 %copy-start.1 = (bf16[1,320,3456]{2,1,0:T(8,128)(2,1)S(1)}, bf16[1,320,3456]{2,1,0:T(8,128)(2,1)}, u32[]{:S(2)}) copy-start(bf16[1,320,3456]{2,1,0:T(8,128)(2,1)} %param.25) | copy-start | bytes 6635524
  408.6 3.4 collective-permute-start.1
  412.9 13.3 %all-to-all-start.10 = ((bf16[16,16,320]{2,0,1:T(8,128)(2,1)}), bf16[16,16,320]{2,0,1:T(8,128)(2,1)S(1)}, u32[]{:S(2)}, u32[]{:S(2)}) async-start(bf16[16,16,320]{2,0,1:T(8,128)(2,1)} %copy.69), calls=%async_computation.10 | async-start | bytes 393216 | tf_op jit(solution)/shard_map/all_to_all | solution.py:105
  417.7 164.8 %all-gather.5.cloned.1.call-start = ((), (), s32[]{:S(2)}) async-start(), calls=%async_computation.17 | async-start | bytes 3760128 | tf_op jit(solution)/shard_map/all_gather | solution.py:43
  480.9 60.6 %all-to-all-start.5 = ((bf16[16,256,216]{1,2,0:T(8,128)(2,1)}), bf16[16,256,216]{1,2,0:T(8,128)(2,1)}, u32[]{:S(2)}, u32[]{:S(2)}) async-start(bf16[16,256,216]{1,2,0:T(8,128)(2,1)} %broadcast_in_dim.30), calls=%async_computation.5 | async-start | bytes 3538944 | tf_op jit(solution)/shard_map/all_to_all | solution.py:22
  542.6 34.1 %all-to-all-start.6 = ((bf16[8,256,320]{1,2,0:T(8,128)(2,1)}), bf16[8,256,320]{1,2,0:T(8,128)(2,1)S(1)}, u32[]{:S(2)}, u32[]{:S(2)}) async-start(bf16[8,256,320]{1,2,0:T(8,128)(2,1)} %broadcast_in_dim.31), calls=%async_computation.6 | async-start | bytes 2621440 | tf_op jit(solution)/shard_map/all_to_all | solution.py:22
  577.8 13.1 %all-to-all-start.7 = ((bf16[16,16,320]{2,1,0:T(8,128)(2,1)}), bf16[16,16,320]{2,1,0:T(8,128)(2,1)S(1)}, u32[]{:S(2)}, u32[]{:S(2)}) async-start(bf16[16,16,320]{2,1,0:T(8,128)(2,1)} %bitcast.16), calls=%async_computation.7 | async-start | bytes 393216 | tf_op jit(solution)/shard_map/all_to_all | solution.py:122
  582.5 4.2 copy-start.4
  586.7 2.7 copy-start.18
  592.1 22.2 %all-to-all-start.12 = ((bf16[8,256,320]{1,2,0:T(8,128)(2,1)}), bf16[8,256,320]{1,2,0:T(8,128)(2,1)S(1)}, u32[]{:S(2)}, u32[]{:S(2)}) async-start(bf16[8,256,320]{1,2,0:T(8,128)(2,1)} %broadcast_in_dim.34), calls=%async_computation.12 | async-start | bytes 2621440 | tf_op jit(solution)/shard_map/all_to_all | solution.py:22
  597.2 25.2 %copy-start.25 = (bf16[16,5120]{1,0:T(8,128)(2,1)S(1)}, bf16[16,5120]{1,0:T(8,128)(2,1)}, u32[]{:S(2)}) copy-start(bf16[16,5120]{1,0:T(8,128)(2,1)} %copy-done.24) | copy-start | bytes 491524
  614.5 16.1 %copy-start.14 = (bf16[16,5120]{1,0:T(8,128)(2,1)S(1)}, bf16[16,5120]{1,0:T(8,128)(2,1)}, u32[]{:S(2)}) copy-start(bf16[16,5120]{1,0:T(8,128)(2,1)} %param.20) | copy-start | bytes 491524
  615.3 15.0 %all-to-all-start.13 = ((bf16[16,16,320]{2,1,0:T(8,128)(2,1)}), bf16[16,16,320]{2,1,0:T(8,128)(2,1)S(1)}, u32[]{:S(2)}, u32[]{:S(2)}) async-start(bf16[16,16,320]{2,1,0:T(8,128)(2,1)} %bitcast.32), calls=%async_computation.13 | async-start | bytes 393216 | tf_op jit(solution)/shard_map/all_to_all | solution.py:122
  (7 other events, 10.1 us)
Sparse Core Ops, SparseCore 0:
  41.3 77.1 reduce-scatter.6
  220.7 75.7 reduce-scatter.8
  299.1 71.2 all-gather.2
  479.6 101.0 all-gather.4
where the time goes:
time: 640 us; the launch traced here: 638 us
  waiting for transfers between devices  396 us (62%)
  blocking collectives  112 us (18%)
  starting transfers between devices  53.5 us (8%)
  local copies, waits for them, and re-layouts  34.8 us (5%)
  other arithmetic  14.6 us (2%)
  between operations  14.2 us (2%)
  matrix products  12.5 us (2%)
    unnamed x6, waiting for transfers between devices  153 us
    all_to_all x4, waiting for transfers between devices, copy_for_each(): return lax.all_to_all(copies, axis, split_axis=0, concat_axis=0, tiled=True)  135 us
    all_gather x2, waiting for transfers between devices, turned_gather(): out, at, done = (lax.all_gather(both, axis, axis=0, tiled=True), 0, [])  71.4 us
    all_to_all x1, blocking collectives, sent_and_summed(): lax.all_to_all(blocks, axis, split_axis=0, concat_axis=0, tiled=True)  46 us
    all_to_all x2, blocking collectives, copy_for_each(): return lax.all_to_all(copies, axis, split_axis=0, concat_axis=0, tiled=True)  40.3 us
    all_to_all x2, blocking collectives, sum_back(): lax.all_to_all(summed.astype(jnp.bfloat16), 'dp', split_axis=0, concat_ax...  25.9 us
    all_to_all x3, waiting for transfers between devices, to_columns(): lax.all_to_all(rows_here, 'dp', split_axis=1, concat_axis=0, tiled=True)  25.6 us
    all_to_all x3, starting transfers between devices, to_columns(): lax.all_to_all(rows_here, 'dp', split_axis=1, concat_axis=0, tiled=True)  19.5 us
  transfers between devices with their start and end apart: 15, of which 14 were waited for; matrix products, arithmetic and copies ran while one was open for 2% of the time, Pallas kernels for 0%

commit v1 on v0

v1 whole, which is shorter than its diff:
```python
import functools

import jax
import jax.numpy as jnp
from jax import lax
from jax.experimental import pallas as pl
from jax.experimental.pallas import tpu as pltpu
from jax.sharding import PartitionSpec as P

EPSILON = 1e-06
MESH = pl.DeviceIdType.MESH
F32 = jnp.float32
BF16 = jnp.bfloat16
Z = 8
ORDER = (4, 3, -3, 2, -2, 1, -1, 0)


def halves(tiles):
    first = (tiles + 1) // 2
    return ((0, first * 128, 0), (first * 128, (tiles - first) * 128, 1))


def rows_of(block):
    return block.reshape(-1, block.shape[-1])


def kernel(
    sizes,
    blocks,
    gain_here,
    gain_all,
    wg_hbm,
    wu_hbm,
    wd_hbm,
    acts,
    grads,
    wg,
    wu,
    wd,
    tin,
    pin,
    xg,
    pg,
    pu,
    pd,
    gu_y,
    gu_ring_y,
    gu_ring_z,
    gu_out,
    gu_fin,
    dh_y,
    dh_ring_y,
    dh_ring_z,
    dh_out,
    dh_fin,
    stash_g,
    stash_u,
    dh_sum,
    hid,
    dg,
    du,
    acc,
    t_out,
    t_in,
    made,
    st_out,
    st_in,
    rows_early,
    rows_back,
    rows_last,
    inv,
    w_sem,
    in_sem,
    gu_sem,
    gu_ysem,
    dh_sem,
    dh_ysem,
    ag_sem,
    ag_ysem,
    t_sem,
    p_sem,
    st_sem,
    row_send,
    row_recv,
    fwd_sem,
    go_sem,
):
    dp_count, tensor_count, rows, width, hidden = sizes
    per = dp_count // tensor_count
    tiles = hidden // 128
    cut = ((tiles * 5 + 8) // 9) * 128
    step_cols = 384
    seg = lax.axis_index("segment")
    i = lax.axis_index("dp")
    j = lax.axis_index("tensor")
    y = i // Z
    m = lax.rem(i, Z)
    across = (seg, (1 - y) * Z + m, j)
    side = (
        (seg, y * Z + lax.rem(m + Z - 1, Z), j),
        (seg, y * Z + lax.rem(m + 1, Z), j),
    )
    partner = (1 - seg, i, j)

    def at(offset):
        return lax.rem(m + offset + Z, Z)

    def dp_peer(r):
        return (seg, lax.rem(i + r, dp_count), j)

    def tensor_at(r):
        return lax.rem(j + r, tensor_count)

    def send(src, dst, send_sem, recv_sem, to):
        copy = pltpu.make_async_remote_copy(
            src_ref=src,
            dst_ref=dst,
            send_sem=send_sem,
            recv_sem=recv_sem,
            device_id=to,
            device_id_type=MESH,
        )
        copy.start()
        return copy

    def arrived(ref, sem):
        pltpu.make_async_copy(ref, ref, sem).wait()

    barrier = pltpu.get_barrier_semaphore()
    for r in range(1, dp_count):
        pl.semaphore_signal(barrier, inc=1, device_id=dp_peer(r), device_id_type=MESH)
    for r in range(1, tensor_count):
        pl.semaphore_signal(barrier, inc=1, device_id=(seg, i, tensor_at(r)), device_id_type=MESH)
    pl.semaphore_signal(barrier, inc=1, device_id=partner, device_id_type=MESH)
    loads = [
        pltpu.make_async_copy(src.at[0], dst, w_sem.at[n])
        for n, (src, dst) in enumerate(((wg_hbm, wg), (wu_hbm, wu), (wd_hbm, wd)))
    ]
    for load in loads:
        load.start()
    tin[i] = blocks[i]
    pl.semaphore_wait(barrier, dp_count - 1 + tensor_count - 1 + 1)

    entry = []
    for r in range(1, dp_count):
        to = lax.rem(i + r, dp_count)
        entry.append(
            send(blocks.at[to], tin.at[i], in_sem.at[0, r], in_sem.at[1, r], (seg, to, j))
        )

    def write_inverse(source):
        def add(b, total):
            v = source[b].astype(F32)
            return total + v * v

        squares = lax.fori_loop(0, dp_count, add, jnp.zeros((rows, width), F32))
        mean = jnp.sum(squares, axis=1, keepdims=True) / (dp_count * width)
        inv[...] = jnp.broadcast_to(lax.rsqrt(mean + EPSILON), (rows, 128))

    def spread(x, weight, out, c0, count):
        span = step_cols if count % step_cols == 0 else 128

        def one(n, carry):
            c = pl.multiple_of(c0 + n * span, 128)
            v = jnp.dot(x, weight[:, pl.ds(c, span)], preferred_element_type=F32)
            out[:, :, :, pl.ds(c, span)] = v.astype(BF16).reshape(2, Z, rows, span)
            return carry

        lax.fori_loop(0, count // span, one, 0)

    def fold(left, weight, first):
        span = step_cols

        def one(n, carry):
            c = pl.multiple_of(n * span, 128)
            v = lax.dot_general(
                rows_of(left[:, :, :, pl.ds(c, span)]),
                weight[:, pl.ds(c, span)],
                (((1,), (1,)), ((), ())),
                preferred_element_type=F32,
            )
            acc[...] += v
            return carry

        if first:
            acc[...] = jnp.zeros_like(acc)
        lax.fori_loop(0, hidden // span, one, 0)

    class Ring:
        def __init__(self, own, land, pieces, sem):
            self.own, self.land, self.pieces, self.sem = own, land, pieces, sem
            self.last, self.sent = {}, []

        def cols(self, t, d, k):
            c0, w, _ = self.pieces[k]
            lead = (slice(None),) * (len(self.land.shape) - 3)
            return (t, d, *lead, pl.ds(c0, w))

        def push(self, t, d, k, src):
            copy = send(
                src,
                self.land.at[self.cols(t, d, k)],
                self.sem.at[0, t, d, k],
                self.sem.at[1, t, d, k],
                side[d],
            )
            self.last[t, d, k] = copy
            self.sent.append(copy)

        def step(self, t):
            for k, (c0, w, anti) in enumerate(self.pieces):
                for d in (0, 1):
                    dest = at(t - 4 if d == 0 else 4 - t)
                    if t == 0 and d != anti:
                        continue
                    if t == 0 or (t == 1 and d != anti):
                        self.push(t, d, k, self.own(dest, c0, w))
                        continue
                    self.last[t - 1, d, k].wait_recv()
                    here = self.land.at[self.cols(t - 1, d, k)]
                    here[...] = here[...] + self.own(dest, c0, w)[...]
                    self.push(t, d, k, here)

        def finish(self):
            for k in range(len(self.pieces)):
                for d in (0, 1):
                    self.last[3, d, k].wait_recv()

    def reduce_scatter(py, y0, wy, pz, z0, wz, by, ring_y, ring_z, z_out, z_fin, sem, ysem, fill_y, fill_z):
        fill_y()
        swaps = [
            send(
                py.at[1 - y, at(off), :, pl.ds(y0, wy)],
                by.at[at(off)],
                ysem.at[0, n],
                ysem.at[1, n],
                across,
            )
            for n, off in enumerate(ORDER)
        ]
        fill_z()
        over_z = Ring(
            lambda dest, c0, w: pz.at[:, dest, :, pl.ds(z0 + c0, w)], ring_z, halves(wz // 128), sem.at[0]
        )
        over_y = Ring(lambda dest, c0, w: by.at[dest, :, pl.ds(c0, w)], ring_y, halves(wy // 128), sem.at[1])

        def pair(n):
            swaps[n].wait_recv()
            zd = at(ORDER[n])
            by[zd] = by[zd] + py[y, zd, :, pl.ds(y0, wy)]

        over_z.step(0)
        pair(0)
        over_y.step(0)
        for t in (1, 2, 3):
            over_z.step(t)
            pair(2 * t - 1)
            pair(2 * t)
            over_y.step(t)
        over_z.finish()
        z_out[...] = (
            pz[1 - y, m, :, pl.ds(z0, wz)].astype(F32)
            + ring_z[3, 0, 1 - y].astype(F32)
            + ring_z[3, 1, 1 - y].astype(F32)
        ).astype(BF16)
        last = send(z_out, z_fin, ysem.at[0, Z], ysem.at[1, Z], across)
        pair(7)
        over_y.finish()
        last.wait_recv()
        for copy in (*swaps, *over_z.sent, *over_y.sent, last):
            copy.wait_send()

    def y_total(by, ring_y, c, span):
        cols = pl.ds(c, span)
        return (
            by[m, :, cols].astype(F32) + ring_y[3, 0, :, cols].astype(F32) + ring_y[3, 1, :, cols].astype(F32)
        )

    def z_total(pz, z0, ring_z, z_fin, c, span):
        cols = pl.ds(c, span)
        return (
            pz[y, m, :, pl.ds(z0 + c, span)].astype(F32)
            + ring_z[3, 0, y, :, cols].astype(F32)
            + ring_z[3, 1, y, :, cols].astype(F32)
            + z_fin[:, cols].astype(F32)
        )

    def scatter_hidden_grads(source):
        x = rows_of(source[...])
        reduce_scatter(
            pd, 0, cut, pd, cut, hidden - cut, dh_y, dh_ring_y, dh_ring_z, dh_out, dh_fin, dh_sem, dh_ysem,
            lambda: spread(x, wd, pd, 0, cut),
            lambda: spread(x, wd, pd, cut, hidden - cut),
        )
        dh_sum[:, pl.ds(0, cut)] = y_total(dh_y, dh_ring_y, 0, cut)
        dh_sum[:, pl.ds(cut, hidden - cut)] = z_total(pd, cut, dh_ring_z, dh_fin, 0, hidden - cut)

    def all_gather(a, a0, wa, b, b0, wb, sem, ysem):
        ca, cb = pl.ds(a0, wa), pl.ds(b0, wb)
        sent, over_a, over_b, cross = [], {}, {}, []

        def push_a(t, d, origin):
            part = a.at[y, origin, :, ca]
            over_a[t, d] = send(part, part, sem.at[0, 0, t, d], sem.at[0, 1, t, d], side[d])
            sent.append(over_a[t, d])

        def push_b(t, d, origin):
            part = b.at[:, origin, :, cb]
            over_b[t, d] = send(part, part, sem.at[1, 0, t, d], sem.at[1, 1, t, d], side[d])
            sent.append(over_b[t, d])

        def cross_a(origin):
            part = a.at[y, origin, :, ca]
            n = len(cross)
            cross.append(send(part, part, ysem.at[0, n], ysem.at[1, n], across))

        mine = b.at[y, m, :, cb]
        first = send(mine, mine, ysem.at[0, Z], ysem.at[1, Z], across)
        push_a(0, 0, m)
        push_a(0, 1, m)
        cross_a(m)
        first.wait_recv()
        push_b(0, 0, m)
        push_b(0, 1, m)
        for t in (1, 2, 3, 4):
            for over, push, anti in ((over_a, push_a, 0), (over_b, push_b, 1)):
                for d in (0, 1):
                    if t == 4 and d != anti:
                        continue
                    over[t - 1, d].wait_recv()
                    origin = at(t if d == 0 else -t)
                    if t < 3 or (t == 3 and d == anti):
                        push(t, d, origin)
                    if over is over_a:
                        cross_a(origin)
        for copy in cross:
            copy.wait_recv()
        return [first, *sent, *cross]

    def drain(copies):
        for copy in copies:
            copy.wait_send()

    def tensor_sum(turn):
        t_out[turn] = acc[...].reshape(tensor_count, per, rows, width).astype(BF16)
        copies = []
        for r in range(1, tensor_count):
            jd = tensor_at(r)
            copies.append(
                send(
                    t_out.at[turn, jd],
                    t_in.at[turn, r - 1],
                    t_sem.at[turn, 0, r],
                    t_sem.at[turn, 1, r],
                    (seg, i, jd),
                )
            )
        total = t_out[turn, j].astype(F32)
        for r in range(1, tensor_count):
            copies[r - 1].wait_recv()
            total = total + t_in[turn, r - 1].astype(F32)
        return total, copies

    def to_partner_segment(src):
        copies = []
        for r in range(tensor_count):
            copies.append(
                send(
                    src,
                    pin.at[pl.ds(per * j, per)],
                    p_sem.at[0, r],
                    p_sem.at[1, r],
                    (1 - seg, i, tensor_at(r)),
                )
            )
        return copies

    def from_partner_segment():
        for r in range(tensor_count):
            arrived(pin.at[pl.ds(0, per)], p_sem.at[1, r])

    def to_rows(src, land, kind, to_seg, crosses):
        for r in range(tensor_count):
            for q in range(per):
                to = (to_seg, per * j + q, tensor_at(r))
                s = row_send.at[kind, r, q]
                if crosses or r > 0:
                    send(src.at[q], land.at[i], s, row_recv.at[kind, i], to)
                    continue
                own = i == per * j + q

                @pl.when(own)
                def _():
                    land[i] = src[q]

                @pl.when(jnp.logical_not(own))
                def _():
                    send(src.at[q], land.at[i], s, row_recv.at[kind, i], to)

    def drain_rows(src, kind, crosses):
        for r in range(tensor_count):
            for q in range(per):
                if crosses or r > 0:
                    arrived(src.at[q], row_send.at[kind, r, q])
                    continue

                @pl.when(i != per * j + q)
                def _():
                    arrived(src.at[q], row_send.at[kind, r, q])

    def rows_arrived(land, kind, crosses):
        def one(s, carry):
            if crosses:
                arrived(land.at[s], row_recv.at[kind, s])
            else:

                @pl.when(jnp.logical_or(s != i, i // per != j))
                def _():
                    arrived(land.at[s], row_recv.at[kind, s])

            return carry

        lax.fori_loop(0, dp_count, one, 0)

    early = seg == 0
    late = seg == 1
    here = pl.ds(per * j, per)
    gain_row = gain_here[...]

    for copy in entry:
        copy.wait_recv()

    def scale(source):
        xg[...] = (rows_of(source[...]).astype(F32) * gain_row).astype(BF16)

    @pl.when(early)
    def _():
        scale(tin)

    @pl.when(late)
    def _():
        loads[2].wait()
        pl.semaphore_wait(go_sem, 1)
        scatter_hidden_grads(tin)
        from_partner_segment()
        scale(pin)

    def fill_gate():
        loads[0].wait()
        spread(xg[...], wg, pg, 0, hidden)

    def fill_up():
        loads[1].wait()
        spread(xg[...], wu, pu, 0, hidden)

    reduce_scatter(
        pg, 0, hidden, pu, 0, hidden, gu_y, gu_ring_y, gu_ring_z, gu_out, gu_fin, gu_sem, gu_ysem, fill_gate, fill_up
    )

    @pl.when(early)
    def _():
        write_inverse(blocks)

    @pl.when(late)
    def _():
        rows_arrived(rows_early, 0, True)
        write_inverse(rows_early)

    def activate(n, carry):
        c = pl.multiple_of(n * step_cols, 128)
        cols = pl.ds(c, step_cols)
        factor = inv[:, 0:1]
        gate = factor * y_total(gu_y, gu_ring_y, c, step_cols)
        up = factor * z_total(pu, 0, gu_ring_z, gu_fin, c, step_cols)
        stash_g[:, cols] = gate.astype(BF16)
        stash_u[:, cols] = up.astype(BF16)
        hid[y, m, :, cols] = (gate * jax.nn.sigmoid(gate) * up).astype(BF16)
        return carry

    lax.fori_loop(0, hidden // step_cols, activate, 0)

    def write_hidden_grads():
        def one(n, carry):
            c = pl.multiple_of(n * step_cols, 128)
            cols = pl.ds(c, step_cols)
            g = stash_g[:, cols].astype(F32)
            u = stash_u[:, cols].astype(F32)
            d = dh_sum[:, cols]
            s = jax.nn.sigmoid(g)
            dg[y, m, :, cols] = (d * u * s * (1.0 + g * (1.0 - s))).astype(BF16)
            du[y, m, :, cols] = (d * g * s).astype(BF16)
            return carry

        lax.fori_loop(0, hidden // step_cols, one, 0)

    a_cols = cut
    b_cols = hidden - cut

    def gather_hidden():
        return all_gather(hid, 0, a_cols, hid, a_cols, b_cols, ag_sem.at[0], ag_ysem.at[0])

    def gather_hidden_grads():
        return all_gather(dg, 0, hidden, du, 0, hidden, ag_sem.at[1], ag_ysem.at[1])

    @pl.when(early)
    def _():
        loads[2].wait()
        gathers = gather_hidden()
        pl.semaphore_signal(go_sem, inc=1, device_id=partner, device_id_type=MESH)
        fold(hid, wd, True)
        total, sums = tensor_sum(0)
        made[0] = (tin[here].astype(F32) + total).astype(BF16)
        handed = to_partner_segment(made.at[0])
        to_rows(made.at[0], rows_early, 0, 1 - seg, True)
        drain(gathers)
        drain(sums)
        drain(handed)
        drain_rows(made.at[0], 0, True)
        from_partner_segment()
        scatter_hidden_grads(pin)
        write_hidden_grads()
        gathers = gather_hidden_grads()
        fold(dg, wg, True)
        fold(du, wu, False)
        total, sums = tensor_sum(1)
        made[1] = total.astype(BF16)
        to_rows(made.at[1], rows_last, 2, seg, False)
        arrived(rows_early, fwd_sem.at[1, 0])
        acts[...] = rows_early[...]
        rows_arrived(rows_back, 1, True)
        back = send(rows_back, rows_back, fwd_sem.at[0, 1], fwd_sem.at[1, 1], partner)
        rows_arrived(rows_last, 2, False)
        factor = inv[:, 0:1]
        project = jnp.zeros((rows, width), F32)
        for b in range(dp_count):
            weighted = rows_last[b].astype(F32) * gain_all[b : b + 1, :]
            project = project + weighted * (blocks[b].astype(F32) * factor)
        mean = jnp.sum(project, axis=1, keepdims=True) / (dp_count * width)
        for b in range(dp_count):
            weighted = rows_last[b].astype(F32) * gain_all[b : b + 1, :]
            unit = blocks[b].astype(F32) * factor
            grads[b] = (rows_back[b].astype(F32) + factor * (weighted - unit * mean)).astype(BF16)
        back.wait_send()
        drain(gathers)
        drain(sums)
        drain_rows(made.at[1], 2, False)

    @pl.when(late)
    def _():
        write_hidden_grads()
        gathers = gather_hidden_grads()
        fold(dg, wg, True)
        fold(du, wu, False)
        total, sums = tensor_sum(0)
        weighted = rows_of(total) * gain_row
        e = rows_of(pin[here]).astype(F32)
        count = per * rows
        both = jnp.concatenate([weighted * e, e * e], axis=0)
        st_out[...] = jnp.zeros_like(st_out)
        st_out[:, pl.ds(0, 2 * count)] = lax.dot_general(
            jnp.ones((8, width), F32),
            both,
            (((1,), (1,)), ((), ())),
            preferred_element_type=F32,
            precision=lax.Precision.HIGHEST,
        )
        stats = [
            send(st_out, st_in.at[r], st_sem.at[0, r], st_sem.at[1, r], dp_peer(r)) for r in range(1, dp_count)
        ]
        tally = st_out[...]
        for r in range(1, dp_count):
            stats[r - 1].wait_recv()
            tally = tally + st_in[r]
        turned = tally.T
        dot_e = turned[0:count, 0:1] / (dp_count * width)
        squares = turned[count : 2 * count, 0:1] / (dp_count * width)
        factor = lax.rsqrt(squares + EPSILON)
        c = rows_of(tin[here]).astype(F32)
        d_in = c + factor * (weighted - e * factor * (factor * dot_e))
        made[0] = d_in.astype(BF16).reshape(per, rows, width)
        handed = to_partner_segment(made.at[0])
        to_rows(made.at[0], rows_back, 1, 1 - seg, True)
        drain(gathers)
        drain(sums)
        drain(stats)
        gathers = gather_hidden()
        fold(hid, wd, True)
        total, sums = tensor_sum(1)
        made[1] = (pin[here].astype(F32) + total).astype(BF16)
        to_rows(made.at[1], rows_last, 2, seg, False)
        ahead = send(rows_early, rows_early, fwd_sem.at[0, 0], fwd_sem.at[1, 0], partner)
        arrived(rows_back, fwd_sem.at[1, 1])
        grads[...] = rows_back[...]
        rows_arrived(rows_last, 2, False)
        acts[...] = rows_last[...]
        ahead.wait_send()
        drain(gathers)
        drain(sums)
        drain(handed)
        drain_rows(made.at[0], 1, True)
        drain_rows(made.at[1], 2, False)

    for copy in entry:
        copy.wait_send()


def solution(mesh):
    dp_count, tensor_count = mesh.shape["dp"], mesh.shape["tensor"]

    def body(tokens, cotangent, gains, w_gate, w_up, w_down):
        rows, model = tokens.shape
        _, width, hidden = w_gate.shape
        per = dp_count // tensor_count
        tiles = hidden // 128
        cut = ((tiles * 5 + 8) // 9) * 128
        rest = hidden - cut
        i = lax.axis_index("dp")
        lead = lax.axis_index("segment") == 0

        def in_blocks(a):
            return a.reshape(rows, dp_count, width).transpose(1, 0, 2)

        blocks = in_blocks(jnp.where(lead, tokens, cotangent))
        gain_all = gains.reshape(dp_count, width)
        gain_here = lax.dynamic_slice(gain_all, (i, 0), (1, width))

        def buf(*shape, dtype=BF16):
            return pltpu.VMEM(shape, dtype)

        block = (dp_count, rows, width)
        wide = (2, Z, rows, hidden)
        dma = pltpu.SemaphoreType.DMA
        scratch = [
            buf(width, hidden),
            buf(width, hidden),
            buf(width, hidden),
            buf(*block),
            buf(*block),
            buf(dp_count * rows, width),
            buf(*wide),
            buf(*wide),
            buf(*wide),
            buf(Z, rows, hidden),
            buf(4, 2, rows, hidden),
            buf(4, 2, 2, rows, hidden),
            buf(rows, hidden),
            buf(rows, hidden),
            buf(Z, rows, cut),
            buf(4, 2, rows, cut),
            buf(4, 2, 2, rows, rest),
            buf(rows, rest),
            buf(rows, rest),
            buf(rows, hidden),
            buf(rows, hidden),
            buf(rows, hidden, dtype=F32),
            buf(*wide),
            buf(*wide),
            buf(*wide),
            buf(dp_count * rows, width, dtype=F32),
            buf(2, tensor_count, per, rows, width),
            buf(2, tensor_count - 1, per, rows, width),
            buf(2, per, rows, width),
            buf(8, 128, dtype=F32),
            buf(dp_count, 8, 128, dtype=F32),
            buf(*block),
            buf(*block),
            buf(*block),
            buf(rows, 128, dtype=F32),
            dma((3,)),
            dma((2, dp_count)),
            dma((2, 2, 4, 2, 2)),
            dma((2, Z + 1)),
            dma((2, 2, 4, 2, 2)),
            dma((2, Z + 1)),
            dma((2, 2, 2, 4, 2)),
            dma((2, 2, Z + 1)),
            dma((2, 2, tensor_count)),
            dma((2, tensor_count)),
            dma((2, dp_count)),
            dma((3, tensor_count, per)),
            dma((3, dp_count)),
            dma((2, 2)),
            pltpu.SemaphoreType.REGULAR,
        ]
        vmem = pl.BlockSpec(memory_space=pltpu.VMEM)
        hbm = pl.BlockSpec(memory_space=pl.ANY)
        acts, grads = pl.pallas_call(
            functools.partial(kernel, (dp_count, tensor_count, rows, width, hidden)),
            out_shape=[jax.ShapeDtypeStruct(block, BF16)] * 2,
            in_specs=[vmem, vmem, vmem, hbm, hbm, hbm],
            out_specs=[vmem, vmem],
            scratch_shapes=scratch,
            compiler_params=pltpu.CompilerParams(collective_id=0, has_side_effects=True),
        )(blocks, gain_here, gain_all, w_gate, w_up, w_down)

        def in_rows(a):
            return a.transpose(1, 0, 2).reshape(1, rows, model)

        return in_rows(acts), in_rows(grads)

    in_specs = (
        P("dp", None),
        P("dp", None),
        P("segment", None),
        P("segment", "dp", "tensor"),
        P("segment", "dp", "tensor"),
        P("segment", "dp", "tensor"),
    )
    out_specs = (P("segment", "dp", None), P("segment", "dp", None))
    return jax.shard_map(body, mesh=mesh, in_specs=in_specs, out_specs=out_specs, check_vma=False)
```

time: 640 us -> 235 us (0.37)
  waiting for transfers between devices: 396 us -> 0 us
  Pallas kernels: 0 us -> 225 us
  blocking collectives: 112 us -> 0 us
  starting transfers between devices: 53.5 us -> 0 us
  local copies, waits for them, and re-layouts: 34.8 us -> 5.66 us
  between operations: 14.2 us -> 0.67 us
  matrix products: 12.5 us -> 0 us
  other arithmetic: 14.6 us -> 2.36 us
    pallas_call x0 -> x1, Pallas kernels: none -> 225 us  [body(): pl.pallas_call(functools.partial(kernel, (dp_count, tensor_count, rows, w...]
    all_to_all x9 -> x0, waiting for transfers between devices: 169 us -> none  [the longest x4 135 us: copy_for_each(): return lax.all_to_all(copies, axis, split_axis=0, concat_axis=0, tiled=True)]
    unnamed x6 -> x0, waiting for transfers between devices: 153 us -> none
    all_to_all x5 -> x0, blocking collectives: 112 us -> none  [the longest x1 46 us: sent_and_summed(): lax.all_to_all(blocks, axis, split_axis=0, concat_axis=0, tiled=True)]
    all_gather x2 -> x0, waiting for transfers between devices: 71.4 us -> none  [turned_gather(): out, at, done = (lax.all_gather(both, axis, axis=0, tiled=True), 0, [])]
    all_to_all x9 -> x0, starting transfers between devices: 50.5 us -> none  [the longest x3 19.5 us: to_columns(): lax.all_to_all(rows_here, 'dp', split_axis=1, concat_axis=0, tiled=True)]
    dot_general x6 -> x0, matrix products: 12.5 us -> none  [the longest x3 5.36 us: contract_last(): lax.dot_general(left, right, (((1,), (1,)), ((), ())), preferred_element_...]
    unnamed x42 -> x3, local copies, waits for them, and re-layouts: 11.3 us -> 0.52 us
  transfers between devices with their start and end apart: 15 -> 0, of which waited for: 14 -> 0; matrix products, arithmetic and copies ran while one was open for 2% -> 0% of each run, Pallas kernels for 0% -> 0%
where the time goes in v1:
time: 235 us; the launch traced here: 234 us
  Pallas kernels  225 us (96%)
  local copies, waits for them, and re-layouts  5.66 us (2%)
  other arithmetic  2.36 us (1%)
    pallas_call x1, Pallas kernels, body(): pl.pallas_call(functools.partial(kernel, (dp_count, tensor_count, rows, w...  225 us

profile of v1, /device:TPU:8, one launch (start us, length us, event | category | flops | bytes accessed | tf_op | source)
XLA Modules:
  0.0 234.1 jit_solution(1863264751874538898)
XLA Ops:
  0.6 0.5 broadcast.3
  1.1 1.4 reduce.3
  2.6 0.1 reshape.17.gain_all
  2.6 0.0 copy-start
  2.7 0.6 constant_dynamic-slice_fusion.gain_here
  3.2 0.9 broadcast_select_fusion
  4.2 0.2 reshape.16
  4.3 0.7 copy.12
  5.0 0.0 copy-done
  5.0 225.4 %shard_map.77 = (bf16[16,16,320]{2,1,0:T(8,128)(2,1)}, bf16[16,16,320]{2,1,0:T(8,128)(2,1)}) custom-call(bf16[16,16,320]{2,1,0:T(8,128)(2,1)} %bitcast.5, f32[1,320]{1,0:T(1,128)} %constant_dynamic-slice_fusion.gain_here, f32[16,320]{1,0:T(8,128)} %copy-done, bf16[1,320,3456]{2,1,0:T(8,128)(2,1)} %wg_hbm.1, bf16[1,320,3456]{2,1,0:T(8,128)(2,1)} %wu_hbm.1, ...), custom_call_target="tpu_custom_call" | custom-call | tf_op jit(solution)/shard_map/pallas_call | solution.py:687
  230.4 1.0 copy.9
  231.4 0.8 reshape.18
  232.2 1.0 copy.10
  233.2 0.8 reshape.19
Async XLA Ops:
  2.6 2.4 %copy-start = (f32[16,320]{1,0:T(8,128)}, f32[16,320]{1,0:T(8,128)S(1)}, u32[]{:S(2)}) copy-start(f32[16,320]{1,0:T(8,128)S(1)} %reshape.17.gain_all) | copy-start | bytes 61444

commit v2 on v1

v2 whole, which is shorter than its diff:
```python
import functools

import jax
import jax.numpy as jnp
from jax import lax
from jax.experimental import pallas as pl
from jax.experimental.pallas import tpu as pltpu
from jax.sharding import PartitionSpec as P

EPSILON = 1e-06
MESH = pl.DeviceIdType.MESH
F32 = jnp.float32
BF16 = jnp.bfloat16
Z = 8
ORDER = (4, 3, -3, 2, -2, 1, -1, 0)


def halves(tiles):
    first = (tiles + 1) // 2
    return ((0, first * 128, 0), (first * 128, (tiles - first) * 128, 1))


def rows_of(block):
    return block.reshape(-1, block.shape[-1])


def kernel(
    sizes,
    tokens_hbm,
    cotangent_hbm,
    gains,
    wg_hbm,
    wu_hbm,
    wd_hbm,
    acts,
    grads,
    given,
    blocks,
    gain_all,
    wg,
    wu,
    wd,
    tin,
    pin,
    xg,
    pg,
    pu,
    pd,
    gu_y,
    gu_ring_y,
    gu_ring_z,
    gu_out,
    gu_fin,
    dh_y,
    dh_ring_y,
    dh_ring_z,
    dh_out,
    dh_fin,
    stash_g,
    stash_u,
    dh_sum,
    hid,
    dg,
    du,
    acc,
    t_out,
    t_in,
    made,
    st_out,
    st_in,
    rows_early,
    rows_back,
    rows_last,
    inv,
    w_sem,
    in_sem,
    gu_sem,
    gu_ysem,
    dh_sem,
    dh_ysem,
    ag_sem,
    ag_ysem,
    t_sem,
    p_sem,
    st_sem,
    row_send,
    row_recv,
    fwd_sem,
    go_sem,
):
    dp_count, tensor_count, rows, width, hidden = sizes
    per = dp_count // tensor_count
    tiles = hidden // 128
    cut = ((tiles * 5 + 8) // 9) * 128
    step_cols = 384
    seg = lax.axis_index("segment")
    i = lax.axis_index("dp")
    j = lax.axis_index("tensor")
    y = i // Z
    m = lax.rem(i, Z)
    across = (seg, (1 - y) * Z + m, j)
    side = (
        (seg, y * Z + lax.rem(m + Z - 1, Z), j),
        (seg, y * Z + lax.rem(m + 1, Z), j),
    )
    partner = (1 - seg, i, j)

    def at(offset):
        return lax.rem(m + offset + Z, Z)

    def dp_peer(r):
        return (seg, lax.rem(i + r, dp_count), j)

    def tensor_at(r):
        return lax.rem(j + r, tensor_count)

    def send(src, dst, send_sem, recv_sem, to):
        copy = pltpu.make_async_remote_copy(
            src_ref=src,
            dst_ref=dst,
            send_sem=send_sem,
            recv_sem=recv_sem,
            device_id=to,
            device_id_type=MESH,
        )
        copy.start()
        return copy

    def arrived(ref, sem):
        pltpu.make_async_copy(ref, ref, sem).wait()

    barrier = pltpu.get_barrier_semaphore()
    for r in range(1, dp_count):
        pl.semaphore_signal(barrier, inc=1, device_id=dp_peer(r), device_id_type=MESH)
    for r in range(1, tensor_count):
        pl.semaphore_signal(barrier, inc=1, device_id=(seg, i, tensor_at(r)), device_id_type=MESH)
    pl.semaphore_signal(barrier, inc=1, device_id=partner, device_id_type=MESH)
    loads = [
        pltpu.make_async_copy(src.at[0], dst, w_sem.at[n])
        for n, (src, dst) in enumerate(((wg_hbm, wg), (wu_hbm, wu), (wd_hbm, wd)))
    ]
    early = seg == 0
    late = seg == 1
    take_tokens = pltpu.make_async_copy(tokens_hbm, given, w_sem.at[3])
    take_cotangent = pltpu.make_async_copy(cotangent_hbm, given, w_sem.at[3])

    @pl.when(early)
    def _():
        take_tokens.start()
        take_tokens.wait()

    @pl.when(late)
    def _():
        take_cotangent.start()
        take_cotangent.wait()

    for load in loads:
        load.start()
    for b in range(dp_count):
        span = slice(b * width, (b + 1) * width)
        blocks[b] = given[:, span]
        gain_all[b : b + 1, :] = gains[:, span]
    tin[i] = blocks[i]
    with jax.named_scope("barrier"):
        pl.semaphore_wait(barrier, dp_count - 1 + tensor_count - 1 + 1)

    @pl.when(late)
    def _():
        pl.semaphore_wait(go_sem, 1)

    entry = []
    for r in range(1, dp_count):
        to = lax.rem(i + r, dp_count)
        entry.append(
            send(blocks.at[to], tin.at[i], in_sem.at[0, r], in_sem.at[1, r], (seg, to, j))
        )

    def write_inverse(source):
        def add(b, total):
            v = source[b].astype(F32)
            return total + v * v

        squares = lax.fori_loop(0, dp_count, add, jnp.zeros((rows, width), F32))
        mean = jnp.sum(squares, axis=1, keepdims=True) / (dp_count * width)
        inv[...] = jnp.broadcast_to(lax.rsqrt(mean + EPSILON), (rows, 128))

    def best_span(count, most):
        n = count // 128
        return max(k for k in range(1, n + 1) if n % k == 0 and k * 128 <= most) * 128

    @jax.named_scope("spread")
    def spread(x, weight, out, c0, count):
        span = best_span(count, 1792)

        def one(n, carry):
            c = pl.multiple_of(c0 + n * span, 128)
            v = jnp.dot(x, weight[:, pl.ds(c, span)], preferred_element_type=F32)
            out[:, :, :, pl.ds(c, span)] = v.astype(BF16).reshape(2, Z, rows, span)
            return carry

        if count == span:
            one(0, 0)
        else:
            lax.fori_loop(0, count // span, one, 0)

    @jax.named_scope("fold")
    def fold(left, weight, c0, count, first):
        span = best_span(count, 1152)

        def product(c):
            return lax.dot_general(
                rows_of(left[:, :, :, pl.ds(c, span)]),
                weight[:, pl.ds(c, span)],
                (((1,), (1,)), ((), ())),
                preferred_element_type=F32,
            )

        def one(n, carry):
            acc[...] += product(pl.multiple_of(c0 + n * span, 128))
            return carry

        if first:
            acc[...] = product(c0)
        lax.fori_loop(1 if first else 0, count // span, one, 0)

    class Ring:
        def __init__(self, own, land, pieces, sem):
            self.own, self.land, self.pieces, self.sem = own, land, pieces, sem
            self.last, self.sent = {}, []

        def cols(self, t, d, k):
            c0, w, _ = self.pieces[k]
            lead = (slice(None),) * (len(self.land.shape) - 3)
            return (t, d, *lead, pl.ds(c0, w))

        def push(self, t, d, k, src):
            copy = send(
                src,
                self.land.at[self.cols(t, d, k)],
                self.sem.at[0, t, d, k],
                self.sem.at[1, t, d, k],
                side[d],
            )
            self.last[t, d, k] = copy
            self.sent.append(copy)

        def dest(self, t, d):
            return at(t - 4 if d == 0 else 4 - t)

        def free(self, t, k):
            c0, w, anti = self.pieces[k]
            d = anti if t == 0 else 1 - anti
            self.push(t, d, k, self.own(self.dest(t, d), c0, w))

        def step(self, t):
            for k, (c0, w, anti) in enumerate(self.pieces):
                for d in (0, 1):
                    if t == 1 and d != anti:
                        continue
                    self.last[t - 1, d, k].wait_recv()
                    here = self.land.at[self.cols(t - 1, d, k)]
                    here[...] = here[...] + self.own(self.dest(t, d), c0, w)[...]
                    self.push(t, d, k, here)

        def finish(self, k):
            for d in (0, 1):
                self.last[3, d, k].wait_recv()

    def reduce_scatter(py, y0, wy, pz, z0, wz, by, ring_y, ring_z, z_out, z_fin, sem, ysem, fill_y, fill_z, aside):
        over_z = Ring(
            lambda dest, c0, w: pz.at[:, dest, :, pl.ds(z0 + c0, w)], ring_z, halves(wz // 128), sem.at[0]
        )
        over_y = Ring(lambda dest, c0, w: by.at[dest, :, pl.ds(c0, w)], ring_y, halves(wy // 128), sem.at[1])
        for k, (c0, w, _) in enumerate(over_z.pieces):
            fill_z(z0 + c0, w)
            over_z.free(0, k)
            over_z.free(1, k)
        for c0, w, _ in over_y.pieces:
            fill_y(y0 + c0, w)
        swaps = [
            send(
                py.at[1 - y, at(off), :, pl.ds(y0, wy)],
                by.at[at(off)],
                ysem.at[0, n],
                ysem.at[1, n],
                across,
            )
            for n, off in enumerate(ORDER)
        ]

        def pair(n):
            swaps[n].wait_recv()
            zd = at(ORDER[n])
            by[zd] = by[zd] + py[y, zd, :, pl.ds(y0, wy)]

        aside()

        def step_z(t):
            with jax.named_scope("z%d" % t):
                over_z.step(t)

        def step_y(t):
            with jax.named_scope("y%d" % t):
                over_y.step(t)

        step_z(1)
        pair(0)
        for k in (0, 1):
            over_y.free(0, k)
        step_z(2)
        pair(1)
        pair(2)
        for k in (0, 1):
            over_y.free(1, k)
        step_y(1)
        step_z(3)
        pair(3)
        pair(4)
        step_y(2)
        ends = []
        for k, (c0, w, _) in enumerate(over_z.pieces):
            with jax.named_scope("zf"):
                over_z.finish(k)
            cols = pl.ds(c0, w)
            z_out[:, cols] = (
                pz[1 - y, m, :, pl.ds(z0 + c0, w)].astype(F32)
                + ring_z[3, 0, 1 - y, :, cols].astype(F32)
                + ring_z[3, 1, 1 - y, :, cols].astype(F32)
            ).astype(BF16)
            ends.append(
                send(z_out.at[:, cols], z_fin.at[:, cols], ysem.at[0, Z + k], ysem.at[1, Z + k], across)
            )
        pair(5)
        pair(6)
        step_y(3)
        pair(7)
        with jax.named_scope("yf"):
            over_y.finish(0)
            over_y.finish(1)
        with jax.named_scope("last"):
            for copy in ends:
                copy.wait_recv()
        for copy in (*swaps, *over_z.sent, *over_y.sent, *ends):
            copy.wait_send()

    def y_total(by, ring_y, c, span):
        cols = pl.ds(c, span)
        return (
            by[m, :, cols].astype(F32) + ring_y[3, 0, :, cols].astype(F32) + ring_y[3, 1, :, cols].astype(F32)
        )

    def z_total(pz, z0, ring_z, z_fin, c, span):
        cols = pl.ds(c, span)
        return (
            pz[y, m, :, pl.ds(z0 + c, span)].astype(F32)
            + ring_z[3, 0, y, :, cols].astype(F32)
            + ring_z[3, 1, y, :, cols].astype(F32)
            + z_fin[:, cols].astype(F32)
        )

    @jax.named_scope("rs_dh")
    def scatter_hidden_grads(source, aside):
        x = rows_of(source[...])
        reduce_scatter(
            pd, 0, cut, pd, cut, hidden - cut, dh_y, dh_ring_y, dh_ring_z, dh_out, dh_fin, dh_sem, dh_ysem,
            lambda c, w: spread(x, wd, pd, c, w),
            lambda c, w: spread(x, wd, pd, c, w),
            aside,
        )
        dh_sum[:, pl.ds(0, cut)] = y_total(dh_y, dh_ring_y, 0, cut)
        dh_sum[:, pl.ds(cut, hidden - cut)] = z_total(pd, cut, dh_ring_z, dh_fin, 0, hidden - cut)

    def all_gather(a, a0, wa, b, b0, wb, sem, ysem, between):
        ca, cb = pl.ds(a0, wa), pl.ds(b0, wb)
        sent, over_a, over_b, cross = [], {}, {}, []

        def part(c0, w, t, d):
            if t < 3:
                return pl.ds(c0, w)
            h0, hw, _ = halves(w // 128)[d]
            return pl.ds(c0 + h0, hw)

        def push_a(t, d, origin):
            piece = a.at[y, origin, :, part(a0, wa, t, d)]
            over_a[t, d] = send(piece, piece, sem.at[0, 0, t, d], sem.at[0, 1, t, d], side[d])
            sent.append(over_a[t, d])

        def push_b(t, d, yy, origin):
            piece = b.at[yy, origin, :, part(b0, wb, t, d)]
            n = 1 if yy is y else 2
            over_b[n, t, d] = send(piece, piece, sem.at[n, 0, t, d], sem.at[n, 1, t, d], side[d])
            sent.append(over_b[n, t, d])

        def cross_a(origin):
            piece = a.at[y, origin, :, ca]
            n = len(cross)
            cross.append(send(piece, piece, ysem.at[0, n], ysem.at[1, n], across))

        def arrive_a(t):
            with jax.named_scope("A%d" % t):
                for d in (0, 1):
                    over_a[t - 1, d].wait_recv()
                    origin = at(t if d == 0 else -t)
                    if t < 4:
                        push_a(t, d, origin)
                        cross_a(origin)
                if t == 4:
                    cross_a(at(4))

        other = 1 - y

        def arrive_b(t, yy):
            n = 1 if yy is y else 2
            with jax.named_scope("%s%d" % (" bB"[n], t)):
                for d in (0, 1):
                    over_b[n, t - 1, d].wait_recv()
                    if t < 4:
                        push_b(t, d, yy, at(t if d == 0 else -t))

        mine = b.at[y, m, :, cb]
        first = send(mine, mine, ysem.at[0, Z], ysem.at[1, Z], across)
        push_a(0, 0, m)
        push_a(0, 1, m)
        push_b(0, 0, y, m)
        push_b(0, 1, y, m)
        cross_a(m)
        for t in (1, 2, 3, 4):
            arrive_a(t)
            if t == 1:
                with jax.named_scope("first"):
                    first.wait_recv()
                push_b(0, 0, other, m)
                push_b(0, 1, other, m)
            else:
                arrive_b(t - 1, other)
            if t < 4:
                arrive_b(t, y)
        with jax.named_scope("cross"):
            for copy in cross:
                copy.wait_recv()
        between()
        arrive_b(4, y)
        arrive_b(4, other)
        return [first, *sent, *cross]

    def drain(copies):
        for copy in copies:
            copy.wait_send()

    def row_block(turn, jd, q):
        if turn == 0 or per != 2:
            return per * jd + q
        return lax.rem(i + jd if q == 0 else i - 1 - jd + dp_count, dp_count)

    @jax.named_scope("tsum")
    def tensor_sum(turn):
        t_out[turn] = acc[...].reshape(dp_count, rows, width).astype(BF16)
        copies = {}
        for r in range(1, tensor_count):
            jd = tensor_at(r)
            for q in range(per):
                copies[r, q] = send(
                    t_out.at[turn, row_block(turn, jd, q)],
                    t_in.at[turn, r - 1, q],
                    t_sem.at[turn, 0, r, q],
                    t_sem.at[turn, 1, r, q],
                    (seg, i, jd),
                )
        totals = [t_out[turn, row_block(turn, j, q)].astype(F32) for q in range(per)]
        for r in range(1, tensor_count):
            for q in range(per):
                copies[r, q].wait_recv()
                totals[q] = totals[q] + t_in[turn, r - 1, q].astype(F32)
        return totals, list(copies.values())

    def to_partner_segment(src):
        copies = []
        for r in range(tensor_count):
            copies.append(
                send(
                    src,
                    pin.at[pl.ds(per * j, per)],
                    p_sem.at[0, r],
                    p_sem.at[1, r],
                    (1 - seg, i, tensor_at(r)),
                )
            )
        return copies

    @jax.named_scope("wait_seg")
    def from_partner_segment():
        for r in range(tensor_count):
            arrived(pin.at[pl.ds(0, per)], p_sem.at[1, r])

    @jax.named_scope("exchange")
    def exchange(land, kind):
        land[i] = pin[i]
        return [
            send(
                pin.at[lax.rem(i + r, dp_count)],
                land.at[i],
                row_send.at[kind, r],
                row_recv.at[kind, i],
                dp_peer(r),
            )
            for r in range(1, dp_count)
        ]

    @jax.named_scope("exchanged")
    def exchanged(land, kind):
        def one(r, carry):
            s = lax.rem(i + r, dp_count)
            arrived(land.at[s], row_recv.at[kind, s])
            return carry

        lax.fori_loop(1, dp_count, one, 0)

    def mine_too(q):
        return row_block(1, j, q) == i

    @jax.named_scope("to_rows")
    def to_rows(src, land):
        for r in range(tensor_count):
            for q in range(per):
                to = (seg, row_block(1, j, q), tensor_at(r))
                s = row_send.at[2, r * per + q]
                if r > 0:
                    send(src.at[q], land.at[i], s, row_recv.at[2, i], to)
                    continue

                @pl.when(mine_too(q))
                def _():
                    land[i] = src[q]

                @pl.when(jnp.logical_not(mine_too(q)))
                def _():
                    send(src.at[q], land.at[i], s, row_recv.at[2, i], to)

    def drain_rows(src):
        for r in range(tensor_count):
            for q in range(per):
                if r > 0:
                    arrived(src.at[q], row_send.at[2, r * per + q])
                    continue

                @pl.when(jnp.logical_not(mine_too(q)))
                def _():
                    arrived(src.at[q], row_send.at[2, r * per + q])

    @jax.named_scope("rows_wait")
    def rows_arrived(land):
        own = mine_too(0)
        for q in range(1, per):
            own = jnp.logical_or(own, mine_too(q))

        def one(r, carry):
            s = lax.rem(i + r, dp_count)
            arrived(land.at[s], row_recv.at[2, s])
            return carry

        lax.fori_loop(1, dp_count, one, 0)

        @pl.when(jnp.logical_not(own))
        def _():
            arrived(land.at[i], row_recv.at[2, i])

    here = pl.ds(per * j, per)
    gain_row = gain_all[pl.ds(i, 1), :]

    with jax.named_scope("entry_wait"):
        for copy in entry:
            copy.wait_recv()

    def scale(source):
        xg[...] = (rows_of(source[...]).astype(F32) * gain_row).astype(BF16)

    @pl.when(early)
    def _():
        pl.semaphore_signal(go_sem, inc=1, device_id=partner, device_id_type=MESH)
        scale(tin)

    @pl.when(late)
    def _():
        loads[2].wait()
        pl.semaphore_wait(go_sem, 1)
        scatter_hidden_grads(tin, lambda: None)
        from_partner_segment()
        scale(pin)

    loads[0].wait()
    loads[1].wait()

    def hand_early_rows():
        @pl.when(late)
        def _():
            exchange(rows_early, 0)

    def drain_exchange(land, kind):
        for r in range(1, dp_count):
            arrived(land.at[0], row_send.at[kind, r])

    with jax.named_scope("rs_gu"):
        reduce_scatter(
            pg, 0, hidden, pu, 0, hidden, gu_y, gu_ring_y, gu_ring_z, gu_out, gu_fin, gu_sem, gu_ysem,
            lambda c, w: spread(xg[...], wg, pg, c, w),
            lambda c, w: spread(xg[...], wu, pu, c, w),
            hand_early_rows,
        )

    @pl.when(early)
    def _():
        write_inverse(blocks)

    @pl.when(late)
    def _():
        exchanged(rows_early, 0)
        write_inverse(rows_early)

    def activate(n, carry):
        c = pl.multiple_of(n * step_cols, 128)
        cols = pl.ds(c, step_cols)
        factor = inv[:, 0:1]
        gate = factor * y_total(gu_y, gu_ring_y, c, step_cols)
        up = factor * z_total(pu, 0, gu_ring_z, gu_fin, c, step_cols)
        stash_g[:, cols] = gate.astype(BF16)
        stash_u[:, cols] = up.astype(BF16)
        hid[y, m, :, cols] = (gate * jax.nn.sigmoid(gate) * up).astype(BF16)
        return carry

    lax.fori_loop(0, hidden // step_cols, activate, 0)

    def put_rows(out, source):
        for b in range(dp_count):
            out[0, :, b * width : (b + 1) * width] = source[b]

    def write_hidden_grads():
        def one(n, carry):
            c = pl.multiple_of(n * step_cols, 128)
            cols = pl.ds(c, step_cols)
            g = stash_g[:, cols].astype(F32)
            u = stash_u[:, cols].astype(F32)
            d = dh_sum[:, cols]
            s = jax.nn.sigmoid(g)
            dg[y, m, :, cols] = (d * u * s * (1.0 + g * (1.0 - s))).astype(BF16)
            du[y, m, :, cols] = (d * g * s).astype(BF16)
            return carry

        lax.fori_loop(0, hidden // step_cols, one, 0)

    a_cols = cut
    b_cols = hidden - cut

    @jax.named_scope("ag_hid")
    def gather_hidden():
        sent = all_gather(
            hid, 0, a_cols, hid, a_cols, b_cols, ag_sem.at[0], ag_ysem.at[0],
            lambda: fold(hid, wd, 0, a_cols, True),
        )
        fold(hid, wd, a_cols, b_cols, False)
        return sent

    @jax.named_scope("ag_dgu")
    def gather_hidden_grads():
        sent = all_gather(
            dg, 0, hidden, du, 0, hidden, ag_sem.at[1], ag_ysem.at[1],
            lambda: fold(dg, wg, 0, hidden, True),
        )
        fold(du, wu, 0, hidden, False)
        return sent

    @pl.when(early)
    def _():
        loads[2].wait()
        pl.semaphore_signal(go_sem, inc=1, device_id=partner, device_id_type=MESH)
        gathers = gather_hidden()
        totals, sums = tensor_sum(0)
        for q in range(per):
            made[0, q] = (tin[row_block(0, j, q)].astype(F32) + totals[q]).astype(BF16)
        handed = to_partner_segment(made.at[0])
        drain(gathers)
        drain(sums)
        drain(handed)
        from_partner_segment()
        scatter_hidden_grads(pin, lambda: exchange(rows_back, 1))
        write_hidden_grads()
        gathers = gather_hidden_grads()
        exchanged(rows_back, 1)
        back = send(rows_back, rows_back, fwd_sem.at[0, 1], fwd_sem.at[1, 1], partner)
        totals, sums = tensor_sum(1)
        for q in range(per):
            made[1, q] = totals[q].astype(BF16)
        to_rows(made.at[1], rows_last)
        arrived(rows_early, fwd_sem.at[1, 0])
        put_rows(acts, rows_early)
        rows_arrived(rows_last)
        factor = inv[:, 0:1]
        project = jnp.zeros((rows, width), F32)
        for b in range(dp_count):
            weighted = rows_last[b].astype(F32) * gain_all[b : b + 1, :]
            project = project + weighted * (blocks[b].astype(F32) * factor)
        mean = jnp.sum(project, axis=1, keepdims=True) / (dp_count * width)
        for b in range(dp_count):
            weighted = rows_last[b].astype(F32) * gain_all[b : b + 1, :]
            unit = blocks[b].astype(F32) * factor
            grads[0, :, b * width : (b + 1) * width] = (rows_back[b].astype(F32) + factor * (weighted - unit * mean)).astype(BF16)
        back.wait_send()
        drain(gathers)
        drain(sums)
        drain_rows(made.at[1])
        drain_exchange(rows_back, 1)

    @pl.when(late)
    def _():
        write_hidden_grads()
        gathers = gather_hidden_grads()
        totals, sums = tensor_sum(0)
        weighted = jnp.concatenate(totals, axis=0) * gain_row
        e = rows_of(pin[here]).astype(F32)
        count = per * rows
        both = jnp.concatenate([weighted * e, e * e], axis=0)
        st_out[...] = jnp.zeros_like(st_out)
        st_out[:, pl.ds(0, 2 * count)] = lax.dot_general(
            jnp.ones((8, width), F32),
            both,
            (((1,), (1,)), ((), ())),
            preferred_element_type=F32,
            precision=lax.Precision.HIGHEST,
        )
        stats = [
            send(st_out, st_in.at[r], st_sem.at[0, r], st_sem.at[1, r], dp_peer(r)) for r in range(1, dp_count)
        ]
        tally = st_out[...]
        for r in range(1, dp_count):
            with jax.named_scope("st"):
                stats[r - 1].wait_recv()
            tally = tally + st_in[r]
        turned = tally.T
        dot_e = turned[0:count, 0:1] / (dp_count * width)
        squares = turned[count : 2 * count, 0:1] / (dp_count * width)
        factor = lax.rsqrt(squares + EPSILON)
        c = rows_of(tin[here]).astype(F32)
        d_in = c + factor * (weighted - e * factor * (factor * dot_e))
        made[0] = d_in.astype(BF16).reshape(per, rows, width)
        handed = to_partner_segment(made.at[0])
        drain(gathers)
        drain(sums)
        drain(stats)
        gathers = gather_hidden()
        totals, sums = tensor_sum(1)
        for q in range(per):
            made[1, q] = (pin[row_block(1, j, q)].astype(F32) + totals[q]).astype(BF16)
        to_rows(made.at[1], rows_last)
        ahead = send(rows_early, rows_early, fwd_sem.at[0, 0], fwd_sem.at[1, 0], partner)
        arrived(rows_back, fwd_sem.at[1, 1])
        put_rows(grads, rows_back)
        rows_arrived(rows_last)
        put_rows(acts, rows_last)
        ahead.wait_send()
        drain(gathers)
        drain(sums)
        drain(handed)
        drain_rows(made.at[1])
        drain_exchange(rows_early, 0)

    for copy in entry:
        copy.wait_send()


def solution(mesh):
    dp_count, tensor_count = mesh.shape["dp"], mesh.shape["tensor"]

    def body(tokens, cotangent, gains, w_gate, w_up, w_down):
        rows, model = tokens.shape
        _, width, hidden = w_gate.shape
        per = dp_count // tensor_count
        tiles = hidden // 128
        cut = ((tiles * 5 + 8) // 9) * 128
        rest = hidden - cut
        def buf(*shape, dtype=BF16):
            return pltpu.VMEM(shape, dtype)

        block = (dp_count, rows, width)
        wide = (2, Z, rows, hidden)
        dma = pltpu.SemaphoreType.DMA
        scratch = [
            buf(rows, model),
            buf(*block),
            buf(dp_count, width, dtype=F32),
            buf(width, hidden),
            buf(width, hidden),
            buf(width, hidden),
            buf(*block),
            buf(*block),
            buf(dp_count * rows, width),
            buf(*wide),
            buf(*wide),
            buf(*wide),
            buf(Z, rows, hidden),
            buf(4, 2, rows, hidden),
            buf(4, 2, 2, rows, hidden),
            buf(rows, hidden),
            buf(rows, hidden),
            buf(Z, rows, cut),
            buf(4, 2, rows, cut),
            buf(4, 2, 2, rows, rest),
            buf(rows, rest),
            buf(rows, rest),
            buf(rows, hidden),
            buf(rows, hidden),
            buf(rows, hidden, dtype=F32),
            buf(*wide),
            buf(*wide),
            buf(*wide),
            buf(dp_count * rows, width, dtype=F32),
            buf(2, *block),
            buf(2, tensor_count - 1, per, rows, width),
            buf(2, per, rows, width),
            buf(8, 128, dtype=F32),
            buf(dp_count, 8, 128, dtype=F32),
            buf(*block),
            buf(*block),
            buf(*block),
            buf(rows, 128, dtype=F32),
            dma((4,)),
            dma((2, dp_count)),
            dma((2, 2, 4, 2, 2)),
            dma((2, Z + 2)),
            dma((2, 2, 4, 2, 2)),
            dma((2, Z + 2)),
            dma((2, 3, 2, 4, 2)),
            dma((2, 2, Z + 1)),
            dma((2, 2, tensor_count, per)),
            dma((2, tensor_count)),
            dma((2, dp_count)),
            dma((3, dp_count)),
            dma((3, dp_count)),
            dma((2, 2)),
            pltpu.SemaphoreType.REGULAR,
        ]
        vmem = pl.BlockSpec(memory_space=pltpu.VMEM)
        hbm = pl.BlockSpec(memory_space=pl.ANY)
        acts, grads = pl.pallas_call(
            functools.partial(kernel, (dp_count, tensor_count, rows, width, hidden)),
            out_shape=[jax.ShapeDtypeStruct((1, rows, model), BF16)] * 2,
            in_specs=[hbm, hbm, vmem, hbm, hbm, hbm],
            out_specs=[vmem, vmem],
            scratch_shapes=scratch,
            compiler_params=pltpu.CompilerParams(collective_id=0, has_side_effects=True),
        )(tokens, cotangent, gains, w_gate, w_up, w_down)

        return acts, grads

    in_specs = (
        P("dp", None),
        P("dp", None),
        P("segment", None),
        P("segment", "dp", "tensor"),
        P("segment", "dp", "tensor"),
        P("segment", "dp", "tensor"),
    )
    out_specs = (P("segment", "dp", None), P("segment", "dp", None))
    return jax.shard_map(body, mesh=mesh, in_specs=in_specs, out_specs=out_specs, check_vma=False)
```

time: 235 us -> 201 us (0.86)
  Pallas kernels: 225 us -> 197 us
  local copies, waits for them, and re-layouts: 5.66 us -> 3.18 us
  other arithmetic: 2.36 us -> 0 us
    pallas_call x1, Pallas kernels: 225 us -> 197 us  [body(): pl.pallas_call(functools.partial(kernel, (dp_count, tensor_count, rows, w...]
    unnamed x3 -> x2, local copies, waits for them, and re-layouts: 0.52 us -> 3.18 us
    reshape x5 -> x0, local copies, waits for them, and re-layouts: 2.65 us -> none  [the longest x2 1.7 us: in_rows(): return a.transpose(1, 0, 2).reshape(1, rows, model)]
where the time goes in v2:
time: 201 us; the launch traced here: 200 us
  Pallas kernels  197 us (98%)
  local copies, waits for them, and re-layouts  3.18 us (2%)
    pallas_call x1, Pallas kernels, body(): pl.pallas_call(functools.partial(kernel, (dp_count, tensor_count, rows, w...  197 us

profile of v2, /device:TPU:8, one launch (start us, length us, event | category | flops | bytes accessed | tf_op | source)
XLA Modules:
  0.0 200.3 jit_solution(2002841686083274501)
XLA Ops:
  0.6 196.5 %shard_map.77 = (bf16[1,16,5120]{2,1,0:T(8,128)(2,1)}, bf16[1,16,5120]{2,1,0:T(8,128)(2,1)}) custom-call(bf16[16,5120]{1,0:T(8,128)(2,1)} %tokens_hbm.1, bf16[16,5120]{1,0:T(8,128)(2,1)} %cotangent_hbm.1, f32[1,5120]{1,0:T(1,128)} %gains.1, bf16[1,320,3456]{2,1,0:T(8,128)(2,1)} %wg_hbm.1, bf16[1,320,3456]{2,1,0:T(8,128)(2,1)} %wu_hbm.1, ...), custom_call_target="tpu_custom_call" | custom-call | tf_op jit(solution)/shard_map/pallas_call | solution.py:842
  197.1 1.6 copy.10
  198.7 1.6 copy.11

commit v3 on v2

--- a/solution.py
+++ b/solution.py
@@ -11,6 +11,7 @@
 MESH = pl.DeviceIdType.MESH
 F32 = jnp.float32
 BF16 = jnp.bfloat16
+GU_FAR, DH_FAR, HID_FAR, DGU_FAR = False, False, False, False
 Z = 8
 ORDER = (4, 3, -3, 2, -2, 1, -1, 0)
 
@@ -83,8 +84,7 @@
     t_sem,
     p_sem,
     st_sem,
-    row_send,
-    row_recv,
+    row_sem,
     fwd_sem,
     go_sem,
 ):
@@ -99,11 +99,12 @@
     y = i // Z
     m = lax.rem(i, Z)
     across = (seg, (1 - y) * Z + m, j)
-    side = (
-        (seg, y * Z + lax.rem(m + Z - 1, Z), j),
-        (seg, y * Z + lax.rem(m + 1, Z), j),
-    )
     partner = (1 - seg, i, j)
+
+    def beside(d, steps):
+        return (seg, y * Z + lax.rem(m + (Z - steps if d == 0 else steps), Z), j)
+
+    others = pl.ds(0, dp_count - 1)
 
     def at(offset):
         return lax.rem(m + offset + Z, Z)
@@ -168,12 +169,9 @@
     def _():
         pl.semaphore_wait(go_sem, 1)
 
-    entry = []
     for r in range(1, dp_count):
         to = lax.rem(i + r, dp_count)
-        entry.append(
-            send(blocks.at[to], tin.at[i], in_sem.at[0, r], in_sem.at[1, r], (seg, to, j))
-        )
+        send(blocks.at[to], tin.at[i], in_sem.at[0], in_sem.at[1], (seg, to, j))
 
     def write_inverse(source):
         def add(b, total):
@@ -224,9 +222,9 @@
         lax.fori_loop(1 if first else 0, count // span, one, 0)
 
     class Ring:
-        def __init__(self, own, land, pieces, sem):
-            self.own, self.land, self.pieces, self.sem = own, land, pieces, sem
-            self.last, self.sent = {}, []
+        def __init__(self, own, land, pieces, out_sem, sem, far):
+            self.own, self.land, self.pieces, self.out_sem, self.sem, self.far = own, land, pieces, out_sem, sem, far
+            self.last = {}
 
         def cols(self, t, d, k):
             c0, w, _ = self.pieces[k]
@@ -237,22 +235,29 @@
             copy = send(
                 src,
                 self.land.at[self.cols(t, d, k)],
-                self.sem.at[0, t, d, k],
-                self.sem.at[1, t, d, k],
-                side[d],
+                self.out_sem,
+                self.sem.at[t, d, k],
+                beside(d, 2 if self.far and t in (0, 2) else 1),
             )
             self.last[t, d, k] = copy
-            self.sent.append(copy)
 
         def dest(self, t, d):
             return at(t - 4 if d == 0 else 4 - t)
 
-        def free(self, t, k):
+        def free(self, distance, k):
             c0, w, anti = self.pieces[k]
-            d = anti if t == 0 else 1 - anti
-            self.push(t, d, k, self.own(self.dest(t, d), c0, w))
+            t = 4 - distance
+            for d in (0, 1):
+                if t == 0 and d != anti or t == 1 and d == anti and not self.far:
+                    continue
+                if t == 2 or t == 3 and not self.far:
+                    continue
+                self.push(t, d, k, self.own(self.dest(t, d), c0, w))
 
         def step(self, t):
+            if self.far:
+                self.join(t)
+                return
             for k, (c0, w, anti) in enumerate(self.pieces):
                 for d in (0, 1):
                     if t == 1 and d != anti:
@@ -262,27 +267,51 @@
                     here[...] = here[...] + self.own(self.dest(t, d), c0, w)[...]
                     self.push(t, d, k, here)
 
+        def join(self, t):
+            if t != 2:
+                return
+            for k, (c0, w, anti) in enumerate(self.pieces):
+                for d in (0, 1):
+                    self.last[1, d, k].wait_recv()
+                    here = self.land.at[self.cols(1, d, k)]
+                    total = here[...].astype(F32) + self.own(self.dest(2, d), c0, w)[...].astype(F32)
+                    if d == anti:
+                        self.last[0, d, k].wait_recv()
+                        total = total + self.land[self.cols(0, d, k)].astype(F32)
+                    here[...] = total.astype(BF16)
+                    self.push(2, d, k, here)
+
         def finish(self, k):
             for d in (0, 1):
                 self.last[3, d, k].wait_recv()
-
-    def reduce_scatter(py, y0, wy, pz, z0, wz, by, ring_y, ring_z, z_out, z_fin, sem, ysem, fill_y, fill_z, aside):
+                if self.far:
+                    self.last[2, d, k].wait_recv()
+
+    def ring_total(land, far, *index):
+        total = land[(3, 0, *index)].astype(F32) + land[(3, 1, *index)].astype(F32)
+        if far:
+            total = total + land[(2, 0, *index)].astype(F32) + land[(2, 1, *index)].astype(F32)
+        return total
+
+    def reduce_scatter(py, y0, wy, pz, z0, wz, by, ring_y, ring_z, z_out, z_fin, sem, ysem, fill_y, fill_z, aside, far):
         over_z = Ring(
-            lambda dest, c0, w: pz.at[:, dest, :, pl.ds(z0 + c0, w)], ring_z, halves(wz // 128), sem.at[0]
+            lambda dest, c0, w: pz.at[:, dest, :, pl.ds(z0 + c0, w)], ring_z, halves(wz // 128), ysem.at[1], sem.at[0], far
         )
-        over_y = Ring(lambda dest, c0, w: by.at[dest, :, pl.ds(c0, w)], ring_y, halves(wy // 128), sem.at[1])
+        over_y = Ring(
+            lambda dest, c0, w: by.at[dest, :, pl.ds(c0, w)], ring_y, halves(wy // 128), ysem.at[2], sem.at[1], far
+        )
         for k, (c0, w, _) in enumerate(over_z.pieces):
             fill_z(z0 + c0, w)
-            over_z.free(0, k)
-            over_z.free(1, k)
+            for distance in (4, 3, 1):
+                over_z.free(distance, k)
         for c0, w, _ in over_y.pieces:
             fill_y(y0 + c0, w)
         swaps = [
             send(
                 py.at[1 - y, at(off), :, pl.ds(y0, wy)],
                 by.at[at(off)],
-                ysem.at[0, n],
-                ysem.at[1, n],
+                ysem.at[0],
+                ysem.at[5 + n],
                 across,
             )
             for n, off in enumerate(ORDER)
@@ -306,55 +335,51 @@
         step_z(1)
         pair(0)
         for k in (0, 1):
-            over_y.free(0, k)
+            over_y.free(4, k)
         step_z(2)
         pair(1)
         pair(2)
         for k in (0, 1):
-            over_y.free(1, k)
+            over_y.free(3, k)
         step_y(1)
         step_z(3)
         pair(3)
         pair(4)
         step_y(2)
-        ends = []
         for k, (c0, w, _) in enumerate(over_z.pieces):
             with jax.named_scope("zf"):
                 over_z.finish(k)
             cols = pl.ds(c0, w)
             z_out[:, cols] = (
                 pz[1 - y, m, :, pl.ds(z0 + c0, w)].astype(F32)
-                + ring_z[3, 0, 1 - y, :, cols].astype(F32)
-                + ring_z[3, 1, 1 - y, :, cols].astype(F32)
+                + ring_total(ring_z, far, 1 - y, slice(None), cols)
             ).astype(BF16)
-            ends.append(
-                send(z_out.at[:, cols], z_fin.at[:, cols], ysem.at[0, Z + k], ysem.at[1, Z + k], across)
-            )
+            send(z_out.at[:, cols], z_fin.at[:, cols], ysem.at[3], ysem.at[4], across)
         pair(5)
         pair(6)
+        for k in (0, 1):
+            over_y.free(1, k)
         step_y(3)
         pair(7)
         with jax.named_scope("yf"):
             over_y.finish(0)
             over_y.finish(1)
         with jax.named_scope("last"):
-            for copy in ends:
-                copy.wait_recv()
-        for copy in (*swaps, *over_z.sent, *over_y.sent, *ends):
-            copy.wait_send()
-
-    def y_total(by, ring_y, c, span):
+            arrived(z_fin, ysem.at[4])
+        arrived(by, ysem.at[0])
+        arrived(pz.at[:, pl.ds(0, 7), :, pl.ds(z0, wz)], ysem.at[1])
+        arrived(by.at[pl.ds(0, 7)], ysem.at[2])
+        arrived(z_out, ysem.at[3])
+
+    def y_total(by, ring_y, c, span, far):
         cols = pl.ds(c, span)
-        return (
-            by[m, :, cols].astype(F32) + ring_y[3, 0, :, cols].astype(F32) + ring_y[3, 1, :, cols].astype(F32)
-        )
-
-    def z_total(pz, z0, ring_z, z_fin, c, span):
+        return by[m, :, cols].astype(F32) + ring_total(ring_y, far, slice(None), cols)
+
+    def z_total(pz, z0, ring_z, z_fin, c, span, far):
         cols = pl.ds(c, span)
         return (
             pz[y, m, :, pl.ds(z0 + c, span)].astype(F32)
-            + ring_z[3, 0, y, :, cols].astype(F32)
-            + ring_z[3, 1, y, :, cols].astype(F32)
+            + ring_total(ring_z, far, y, slice(None), cols)
             + z_fin[:, cols].astype(F32)
         )
 
@@ -366,13 +391,14 @@
             lambda c, w: spread(x, wd, pd, c, w),
             lambda c, w: spread(x, wd, pd, c, w),
             aside,
+            DH_FAR,
         )
-        dh_sum[:, pl.ds(0, cut)] = y_total(dh_y, dh_ring_y, 0, cut)
-        dh_sum[:, pl.ds(cut, hidden - cut)] = z_total(pd, cut, dh_ring_z, dh_fin, 0, hidden - cut)
-
-    def all_gather(a, a0, wa, b, b0, wb, sem, ysem, between):
+        dh_sum[:, pl.ds(0, cut)] = y_total(dh_y, dh_ring_y, 0, cut, DH_FAR)
+        dh_sum[:, pl.ds(cut, hidden - cut)] = z_total(pd, cut, dh_ring_z, dh_fin, 0, hidden - cut, DH_FAR)
+
+    def gather_steps(a, a0, wa, b, b0, wb, sem, ysem, far):
         ca, cb = pl.ds(a0, wa), pl.ds(b0, wb)
-        sent, over_a, over_b, cross = [], {}, {}, []
+        over_a, over_b = {}, {}
 
         def part(c0, w, t, d):
             if t < 3:
@@ -382,27 +408,30 @@
 
         def push_a(t, d, origin):
             piece = a.at[y, origin, :, part(a0, wa, t, d)]
-            over_a[t, d] = send(piece, piece, sem.at[0, 0, t, d], sem.at[0, 1, t, d], side[d])
-            sent.append(over_a[t, d])
+            over_a[t, d] = send(piece, piece, ysem.at[0], sem.at[0, t, d], beside(d, 2 if far and t in (1, 3) else 1))
 
         def push_b(t, d, yy, origin):
             piece = b.at[yy, origin, :, part(b0, wb, t, d)]
             n = 1 if yy is y else 2
-            over_b[n, t, d] = send(piece, piece, sem.at[n, 0, t, d], sem.at[n, 1, t, d], side[d])
-            sent.append(over_b[n, t, d])
+            over_b[n, t, d] = send(piece, piece, ysem.at[1], sem.at[n, t, d], beside(d, 2 if far and t in (1, 3) else 1))
+
+        def forwards(t):
+            if far:
+                return (2, 3) if t == 2 else ()
+            return (t,) if t < 4 else ()
 
         def cross_a(origin):
             piece = a.at[y, origin, :, ca]
-            n = len(cross)
-            cross.append(send(piece, piece, ysem.at[0, n], ysem.at[1, n], across))
+            send(piece, piece, ysem.at[2], ysem.at[3], across)
 
         def arrive_a(t):
             with jax.named_scope("A%d" % t):
                 for d in (0, 1):
                     over_a[t - 1, d].wait_recv()
                     origin = at(t if d == 0 else -t)
+                    for later in forwards(t):
+                        push_a(later, d, origin)
                     if t < 4:
-                        push_a(t, d, origin)
                         cross_a(origin)
                 if t == 4:
                     cross_a(at(4))
@@ -414,106 +443,95 @@
             with jax.named_scope("%s%d" % (" bB"[n], t)):
                 for d in (0, 1):
                     over_b[n, t - 1, d].wait_recv()
-                    if t < 4:
-                        push_b(t, d, yy, at(t if d == 0 else -t))
+                    for later in forwards(t):
+                        push_b(later, d, yy, at(t if d == 0 else -t))
 
         mine = b.at[y, m, :, cb]
-        first = send(mine, mine, ysem.at[0, Z], ysem.at[1, Z], across)
-        push_a(0, 0, m)
-        push_a(0, 1, m)
-        push_b(0, 0, y, m)
-        push_b(0, 1, y, m)
+        first = send(mine, mine, ysem.at[4], ysem.at[5], across)
+        starts = (1, 0) if far else (0,)
+        for t in starts:
+            for d in (0, 1):
+                push_a(t, d, m)
+        for t in starts:
+            for d in (0, 1):
+                push_b(t, d, y, m)
         cross_a(m)
+        yield 0
         for t in (1, 2, 3, 4):
             arrive_a(t)
             if t == 1:
                 with jax.named_scope("first"):
                     first.wait_recv()
-                push_b(0, 0, other, m)
-                push_b(0, 1, other, m)
+                for start in starts:
+                    for d in (0, 1):
+                        push_b(start, d, other, m)
             else:
                 arrive_b(t - 1, other)
             if t < 4:
                 arrive_b(t, y)
+                yield t
         with jax.named_scope("cross"):
-            for copy in cross:
-                copy.wait_recv()
-        between()
+            arrived(a.at[0, :, :, ca], ysem.at[3])
+        yield 4
         arrive_b(4, y)
         arrive_b(4, other)
-        return [first, *sent, *cross]
-
-    def drain(copies):
-        for copy in copies:
-            copy.wait_send()
+        yield 5
+
+    def advance(steps, to):
+        while next(steps) != to:
+            pass
+
+    def gathered(a, a0, wa, b, b0, wb, ysem):
+        ca, cb = pl.ds(a0, wa), pl.ds(b0, wb)
+        arrived(a.at[0, pl.ds(0, 7), :, ca], ysem.at[0])
+        arrived(b.at[:, pl.ds(0, 7), :, cb], ysem.at[1])
+        arrived(a.at[0, :, :, ca], ysem.at[2])
+        arrived(b.at[0, 0, :, cb], ysem.at[4])
 
     def row_block(turn, jd, q):
         if turn == 0 or per != 2:
             return per * jd + q
         return lax.rem(i + jd if q == 0 else i - 1 - jd + dp_count, dp_count)
 
-    @jax.named_scope("tsum")
-    def tensor_sum(turn):
+    def tensor_send(turn):
         t_out[turn] = acc[...].reshape(dp_count, rows, width).astype(BF16)
-        copies = {}
         for r in range(1, tensor_count):
             jd = tensor_at(r)
             for q in range(per):
-                copies[r, q] = send(
+                send(
                     t_out.at[turn, row_block(turn, jd, q)],
                     t_in.at[turn, r - 1, q],
-                    t_sem.at[turn, 0, r, q],
-                    t_sem.at[turn, 1, r, q],
+                    t_sem.at[turn, 0],
+                    t_sem.at[turn, 1],
                     (seg, i, jd),
                 )
+
+    @jax.named_scope("tsum")
+    def tensor_sum(turn):
+        arrived(t_in.at[turn], t_sem.at[turn, 1])
         totals = [t_out[turn, row_block(turn, j, q)].astype(F32) for q in range(per)]
         for r in range(1, tensor_count):
             for q in range(per):
-                copies[r, q].wait_recv()
                 totals[q] = totals[q] + t_in[turn, r - 1, q].astype(F32)
-        return totals, list(copies.values())
+        return totals
 
     def to_partner_segment(src):
-        copies = []
         for r in range(tensor_count):
-            copies.append(
-                send(
-                    src,
-                    pin.at[pl.ds(per * j, per)],
-                    p_sem.at[0, r],
-                    p_sem.at[1, r],
-                    (1 - seg, i, tensor_at(r)),
-                )
-            )
-        return copies
+            send(src, pin.at[pl.ds(per * j, per)], p_sem.at[0], p_sem.at[1], (1 - seg, i, tensor_at(r)))
 
     @jax.named_scope("wait_seg")
     def from_partner_segment():
-        for r in range(tensor_count):
-            arrived(pin.at[pl.ds(0, per)], p_sem.at[1, r])
+        arrived(pin, p_sem.at[1])
 
     @jax.named_scope("exchange")
     def exchange(land, kind):
         land[i] = pin[i]
-        return [
-            send(
-                pin.at[lax.rem(i + r, dp_count)],
-                land.at[i],
-                row_send.at[kind, r],
-                row_recv.at[kind, i],
-                dp_peer(r),
-            )
-            for r in range(1, dp_count)
-        ]
+        for r in range(1, dp_count):
+            send(pin.at[lax.rem(i + r, dp_count)], land.at[i], row_sem.at[kind, 0], row_sem.at[kind, 1], dp_peer(r))
 
     @jax.named_scope("exchanged")
     def exchanged(land, kind):
-        def one(r, carry):
-            s = lax.rem(i + r, dp_count)
-            arrived(land.at[s], row_recv.at[kind, s])
-            return carry
-
-        lax.fori_loop(1, dp_count, one, 0)
+        arrived(land.at[others], row_sem.at[kind, 1])
 
     def mine_too(q):
         return row_block(1, j, q) == i
@@ -523,9 +541,9 @@
         for r in range(tensor_count):
             for q in range(per):
                 to = (seg, row_block(1, j, q), tensor_at(r))
-                s = row_send.at[2, r * per + q]
+                out, into = row_sem.at[2, 0], row_sem.at[2, 1]
                 if r > 0:
-                    send(src.at[q], land.at[i], s, row_recv.at[2, i], to)
+                    send(src.at[q], land.at[i], out, into, to)
                     continue
 
                 @pl.when(mine_too(q))
@@ -534,42 +552,30 @@
 
                 @pl.when(jnp.logical_not(mine_too(q)))
                 def _():
-                    send(src.at[q], land.at[i], s, row_recv.at[2, i], to)
-
-    def drain_rows(src):
-        for r in range(tensor_count):
-            for q in range(per):
-                if r > 0:
-                    arrived(src.at[q], row_send.at[2, r * per + q])
-                    continue
-
-                @pl.when(jnp.logical_not(mine_too(q)))
-                def _():
-                    arrived(src.at[q], row_send.at[2, r * per + q])
-
-    @jax.named_scope("rows_wait")
-    def rows_arrived(land):
+                    send(src.at[q], land.at[i], out, into, to)
+
+    def rows_done(land, n):
         own = mine_too(0)
         for q in range(1, per):
             own = jnp.logical_or(own, mine_too(q))
 
-        def one(r, carry):
-            s = lax.rem(i + r, dp_count)
-            arrived(land.at[s], row_recv.at[2, s])
-            return carry
-
-        lax.fori_loop(1, dp_count, one, 0)
+        @pl.when(own)
+        def _():
+            arrived(land.at[others], row_sem.at[2, n])
 
         @pl.when(jnp.logical_not(own))
         def _():
-            arrived(land.at[i], row_recv.at[2, i])
+            arrived(land, row_sem.at[2, n])
+
+    @jax.named_scope("rows_wait")
+    def rows_arrived(land):
+        rows_done(land, 1)
 
     here = pl.ds(per * j, per)
     gain_row = gain_all[pl.ds(i, 1), :]
 
     with jax.named_scope("entry_wait"):
-        for copy in entry:
-            copy.wait_recv()
+        arrived(tin.at[others], in_sem.at[1])
 
     def scale(source):
         xg[...] = (rows_of(source[...]).astype(F32) * gain_row).astype(BF16)
@@ -596,8 +602,7 @@
             exchange(rows_early, 0)
 
     def drain_exchange(land, kind):
-        for r in range(1, dp_count):
-            arrived(land.at[0], row_send.at[kind, r])
+        arrived(land.at[others], row_sem.at[kind, 0])
 
     with jax.named_scope("rs_gu"):
         reduce_scatter(
@@ -605,6 +610,7 @@
             lambda c, w: spread(xg[...], wg, pg, c, w),
             lambda c, w: spread(xg[...], wu, pu, c, w),
             hand_early_rows,
+            GU_FAR,
         )
 
     @pl.when(early)
@@ -620,8 +626,8 @@
         c = pl.multiple_of(n * step_cols, 128)
         cols = pl.ds(c, step_cols)
         factor = inv[:, 0:1]
-        gate = factor * y_total(gu_y, gu_ring_y, c, step_cols)
-        up = factor * z_total(pu, 0, gu_ring_z, gu_fin, c, step_cols)
+        gate = factor * y_total(gu_y, gu_ring_y, c, step_cols, GU_FAR)
+        up = factor * z_total(pu, 0, gu_ring_z, gu_fin, c, step_cols, GU_FAR)
         stash_g[:, cols] = gate.astype(BF16)
         stash_u[:, cols] = up.astype(BF16)
         hid[y, m, :, cols] = (gate * jax.nn.sigmoid(gate) * up).astype(BF16)
@@ -650,43 +656,46 @@
     a_cols = cut
     b_cols = hidden - cut
 
+    hid_args = (hid, 0, a_cols, hid, a_cols, b_cols)
+    dgu_args = (dg, 0, hidden, du, 0, hidden)
+
+    def start_hidden():
+        return gather_steps(*hid_args, ag_sem.at[0], ag_ysem.at[0], HID_FAR)
+
     @jax.named_scope("ag_hid")
-    def gather_hidden():
-        sent = all_gather(
-            hid, 0, a_cols, hid, a_cols, b_cols, ag_sem.at[0], ag_ysem.at[0],
-            lambda: fold(hid, wd, 0, a_cols, True),
-        )
+    def finish_hidden(steps):
+        advance(steps, 4)
+        fold(hid, wd, 0, a_cols, True)
+        advance(steps, 5)
         fold(hid, wd, a_cols, b_cols, False)
-        return sent
 
     @jax.named_scope("ag_dgu")
-    def gather_hidden_grads():
-        sent = all_gather(
-            dg, 0, hidden, du, 0, hidden, ag_sem.at[1], ag_ysem.at[1],
-            lambda: fold(dg, wg, 0, hidden, True),
-        )
+    def gather_hidden_grads(beside_fold):
+        steps = gather_steps(*dgu_args, ag_sem.at[1], ag_ysem.at[1], DGU_FAR)
+        advance(steps, 4)
+        beside_fold()
+        fold(dg, wg, 0, hidden, True)
+        advance(steps, 5)
         fold(du, wu, 0, hidden, False)
-        return sent
 
     @pl.when(early)
     def _():
         loads[2].wait()
         pl.semaphore_signal(go_sem, inc=1, device_id=partner, device_id_type=MESH)
-        gathers = gather_hidden()
-        totals, sums = tensor_sum(0)
+        finish_hidden(start_hidden())
+        tensor_send(0)
+        totals = tensor_sum(0)
         for q in range(per):
             made[0, q] = (tin[row_block(0, j, q)].astype(F32) + totals[q]).astype(BF16)
-        handed = to_partner_segment(made.at[0])
-        drain(gathers)
-        drain(sums)
-        drain(handed)
+        to_partner_segment(made.at[0])
         from_partner_segment()
         scatter_hidden_grads(pin, lambda: exchange(rows_back, 1))
         write_hidden_grads()
-        gathers = gather_hidden_grads()
+        gather_hidden_grads(lambda: None)
+        tensor_send(1)
         exchanged(rows_back, 1)
         back = send(rows_back, rows_back, fwd_sem.at[0, 1], fwd_sem.at[1, 1], partner)
-        totals, sums = tensor_sum(1)
+        totals = tensor_sum(1)
         for q in range(per):
             made[1, q] = totals[q].astype(BF16)
         to_rows(made.at[1], rows_last)
@@ -704,16 +713,16 @@
             unit = blocks[b].astype(F32) * factor
             grads[0, :, b * width : (b + 1) * width] = (rows_back[b].astype(F32) + factor * (weighted - unit * mean)).astype(BF16)
         back.wait_send()
-        drain(gathers)
-        drain(sums)
-        drain_rows(made.at[1])
         drain_exchange(rows_back, 1)
 
     @pl.when(late)
     def _():
         write_hidden_grads()
-        gathers = gather_hidden_grads()
-        totals, sums = tensor_sum(0)
+        steps = start_hidden()
+        gather_hidden_grads(lambda: advance(steps, 0))
+        tensor_send(0)
+        advance(steps, 1)
+        totals = tensor_sum(0)
         weighted = jnp.concatenate(totals, axis=0) * gain_row
         e = rows_of(pin[here]).astype(F32)
         count = per * rows
@@ -726,13 +735,13 @@
             preferred_element_type=F32,
             precision=lax.Precision.HIGHEST,
         )
-        stats = [
-            send(st_out, st_in.at[r], st_sem.at[0, r], st_sem.at[1, r], dp_peer(r)) for r in range(1, dp_count)
-        ]
+        for r in range(1, dp_count):
+            send(st_out, st_in.at[r], st_sem.at[0], st_sem.at[1], dp_peer(r))
+        advance(steps, 2)
+        with jax.named_scope("st"):
+            arrived(st_in.at[pl.ds(1, dp_count - 1)], st_sem.at[1])
         tally = st_out[...]
         for r in range(1, dp_count):
-            with jax.named_scope("st"):
-                stats[r - 1].wait_recv()
             tally = tally + st_in[r]
         turned = tally.T
         dot_e = turned[0:count, 0:1] / (dp_count * width)
@@ -741,12 +750,10 @@
         c = rows_of(tin[here]).astype(F32)
         d_in = c + factor * (weighted - e * factor * (factor * dot_e))
         made[0] = d_in.astype(BF16).reshape(per, rows, width)
-        handed = to_partner_segment(made.at[0])
-        drain(gathers)
-        drain(sums)
-        drain(stats)
-        gathers = gather_hidden()
-        totals, sums = tensor_sum(1)
+        to_partner_segment(made.at[0])
+        finish_hidden(steps)
+        tensor_send(1)
+        totals = tensor_sum(1)
         for q in range(per):
             made[1, q] = (pin[row_block(1, j, q)].astype(F32) + totals[q]).astype(BF16)
         to_rows(made.at[1], rows_last)
@@ -756,14 +763,16 @@
         rows_arrived(rows_last)
         put_rows(acts, rows_last)
         ahead.wait_send()
-        drain(gathers)
-        drain(sums)
-        drain(handed)
-        drain_rows(made.at[1])
         drain_exchange(rows_early, 0)
-
-    for copy in entry:
-        copy.wait_send()
+        arrived(st_in.at[pl.ds(1, dp_count - 1)], st_sem.at[0])
+
+    gathered(*hid_args, ag_ysem.at[0])
+    gathered(*dgu_args, ag_ysem.at[1])
+    for turn in (0, 1):
+        arrived(t_in.at[turn], t_sem.at[turn, 0])
+    arrived(pin, p_sem.at[0])
+    rows_done(rows_last, 0)
+    arrived(blocks.at[others], in_sem.at[0])
 
 
 def solution(mesh):
@@ -822,18 +831,17 @@
             buf(*block),
             buf(rows, 128, dtype=F32),
             dma((4,)),
-            dma((2, dp_count)),
-            dma((2, 2, 4, 2, 2)),
-            dma((2, Z + 2)),
-            dma((2, 2, 4, 2, 2)),
-            dma((2, Z + 2)),
-            dma((2, 3, 2, 4, 2)),
-            dma((2, 2, Z + 1)),
-            dma((2, 2, tensor_count, per)),
-            dma((2, tensor_count)),
-            dma((2, dp_count)),
-            dma((3, dp_count)),
-            dma((3, dp_count)),
+            dma((2,)),
+            dma((2, 4, 2, 2)),
+            dma((5 + Z,)),
+            dma((2, 4, 2, 2)),
+            dma((5 + Z,)),
+            dma((2, 3, 4, 2)),
+            dma((2, 6)),
+            dma((2, 2)),
+            dma((2,)),
+            dma((2,)),
+            dma((3, 2)),
             dma((2, 2)),
             pltpu.SemaphoreType.REGULAR,
         ]

time: 201 us -> 193 us (0.960)
  Pallas kernels: 197 us -> 188 us
    pallas_call x1, Pallas kernels: 197 us -> 188 us  [body(): pl.pallas_call(functools.partial(kernel, (dp_count, tensor_count, rows, w...]
where the time goes in v3:
time: 193 us; the launch traced here: 192 us
  Pallas kernels  188 us (97%)
  local copies, waits for them, and re-layouts  3.18 us (2%)
    pallas_call x1, Pallas kernels, body(): pl.pallas_call(functools.partial(kernel, (dp_count, tensor_count, rows, w...  188 us

profile of v3, /device:TPU:8, one launch (start us, length us, event | category | flops | bytes accessed | tf_op | source)
XLA Modules:
  0.0 192.2 jit_solution(10839124269574683780)
XLA Ops:
  0.6 188.4 %shard_map.77 = (bf16[1,16,5120]{2,1,0:T(8,128)(2,1)}, bf16[1,16,5120]{2,1,0:T(8,128)(2,1)}) custom-call(bf16[16,5120]{1,0:T(8,128)(2,1)} %tokens_hbm.1, bf16[16,5120]{1,0:T(8,128)(2,1)} %cotangent_hbm.1, f32[1,5120]{1,0:T(1,128)} %gains.1, bf16[1,320,3456]{2,1,0:T(8,128)(2,1)} %wg_hbm.1, bf16[1,320,3456]{2,1,0:T(8,128)(2,1)} %wu_hbm.1, ...), custom_call_target="tpu_custom_call" | custom-call | tf_op jit(solution)/shard_map/pallas_call | solution.py:850
  189.0 1.6 copy.10
  190.6 1.6 copy.11

commit v4 on v3

--- a/solution.py
+++ b/solution.py
@@ -11,7 +11,7 @@
 MESH = pl.DeviceIdType.MESH
 F32 = jnp.float32
 BF16 = jnp.bfloat16
-GU_FAR, DH_FAR, HID_FAR, DGU_FAR = False, False, False, False
+GU_FAR, DH_FAR = False, False
 Z = 8
 ORDER = (4, 3, -3, 2, -2, 1, -1, 0)
 
@@ -33,8 +33,9 @@
     wg_hbm,
     wu_hbm,
     wd_hbm,
-    acts,
-    grads,
+    out_early,
+    out_last,
+    out_back,
     given,
     blocks,
     gain_all,
@@ -396,75 +397,72 @@
         dh_sum[:, pl.ds(0, cut)] = y_total(dh_y, dh_ring_y, 0, cut, DH_FAR)
         dh_sum[:, pl.ds(cut, hidden - cut)] = z_total(pd, cut, dh_ring_z, dh_fin, 0, hidden - cut, DH_FAR)
 
-    def gather_steps(a, a0, wa, b, b0, wb, sem, ysem, far):
+    def gather_steps(a, a0, wa, b, b0, wb, sem, ysem):
         ca, cb = pl.ds(a0, wa), pl.ds(b0, wb)
         over_a, over_b = {}, {}
-
-        def part(c0, w, t, d):
-            if t < 3:
-                return pl.ds(c0, w)
-            h0, hw, _ = halves(w // 128)[d]
+        other = 1 - y
+
+        def part(c0, w, k):
+            h0, hw, _ = halves(w // 128)[k]
             return pl.ds(c0 + h0, hw)
 
-        def push_a(t, d, origin):
-            piece = a.at[y, origin, :, part(a0, wa, t, d)]
-            over_a[t, d] = send(piece, piece, ysem.at[0], sem.at[0, t, d], beside(d, 2 if far and t in (1, 3) else 1))
-
-        def push_b(t, d, yy, origin):
-            piece = b.at[yy, origin, :, part(b0, wb, t, d)]
+        def push_a(t, d, k, origin):
+            piece = a.at[y, origin, :, part(a0, wa, k)]
+            over_a[t, d, k] = send(piece, piece, ysem.at[0], sem.at[0, t, d, k], beside(d, 1))
+
+        def push_b(t, d, k, yy, origin):
+            piece = b.at[yy, origin, :, part(b0, wb, k)]
             n = 1 if yy is y else 2
-            over_b[n, t, d] = send(piece, piece, ysem.at[1], sem.at[n, t, d], beside(d, 2 if far and t in (1, 3) else 1))
-
-        def forwards(t):
-            if far:
-                return (2, 3) if t == 2 else ()
-            return (t,) if t < 4 else ()
-
-        def cross_a(origin):
-            piece = a.at[y, origin, :, ca]
+            over_b[n, t, d, k] = send(piece, piece, ysem.at[1], sem.at[n, t, d, k], beside(d, 1))
+
+        def cross_a(origin, k):
+            piece = a.at[y, origin, :, part(a0, wa, k)]
             send(piece, piece, ysem.at[2], ysem.at[3], across)
+
+        def arrive(t, over, push, *cross):
+            for k in (0, 1):
+                for d in (0, 1):
+                    if t == 4 and d != k:
+                        continue
+                    over[t - 1, d, k].wait_recv()
+                    origin = at(t if d == 0 else -t)
+                    if t < 3 or t == 3 and d == k:
+                        push(t, d, k, origin)
+                    for to in cross:
+                        to(origin, k)
 
         def arrive_a(t):
             with jax.named_scope("A%d" % t):
-                for d in (0, 1):
-                    over_a[t - 1, d].wait_recv()
-                    origin = at(t if d == 0 else -t)
-                    for later in forwards(t):
-                        push_a(later, d, origin)
-                    if t < 4:
-                        cross_a(origin)
-                if t == 4:
-                    cross_a(at(4))
-
-        other = 1 - y
+                arrive(t, over_a, push_a, cross_a)
 
         def arrive_b(t, yy):
             n = 1 if yy is y else 2
             with jax.named_scope("%s%d" % (" bB"[n], t)):
-                for d in (0, 1):
-                    over_b[n, t - 1, d].wait_recv()
-                    for later in forwards(t):
-                        push_b(later, d, yy, at(t if d == 0 else -t))
+                arrive(
+                    t,
+                    {key[1:]: copy for key, copy in over_b.items() if key[0] == n},
+                    lambda t, d, k, origin: push_b(t, d, k, yy, origin),
+                )
 
         mine = b.at[y, m, :, cb]
         first = send(mine, mine, ysem.at[4], ysem.at[5], across)
-        starts = (1, 0) if far else (0,)
-        for t in starts:
+        for k in (0, 1):
             for d in (0, 1):
-                push_a(t, d, m)
-        for t in starts:
+                push_a(0, d, k, m)
+        for k in (0, 1):
             for d in (0, 1):
-                push_b(t, d, y, m)
-        cross_a(m)
+                push_b(0, d, k, y, m)
+        for k in (0, 1):
+            cross_a(m, k)
         yield 0
         for t in (1, 2, 3, 4):
             arrive_a(t)
             if t == 1:
                 with jax.named_scope("first"):
                     first.wait_recv()
-                for start in starts:
+                for k in (0, 1):
                     for d in (0, 1):
-                        push_b(start, d, other, m)
+                        push_b(0, d, k, other, m)
             else:
                 arrive_b(t - 1, other)
             if t < 4:
@@ -660,7 +658,7 @@
     dgu_args = (dg, 0, hidden, du, 0, hidden)
 
     def start_hidden():
-        return gather_steps(*hid_args, ag_sem.at[0], ag_ysem.at[0], HID_FAR)
+        return gather_steps(*hid_args, ag_sem.at[0], ag_ysem.at[0])
 
     @jax.named_scope("ag_hid")
     def finish_hidden(steps):
@@ -671,7 +669,7 @@
 
     @jax.named_scope("ag_dgu")
     def gather_hidden_grads(beside_fold):
-        steps = gather_steps(*dgu_args, ag_sem.at[1], ag_ysem.at[1], DGU_FAR)
+        steps = gather_steps(*dgu_args, ag_sem.at[1], ag_ysem.at[1])
         advance(steps, 4)
         beside_fold()
         fold(dg, wg, 0, hidden, True)
@@ -689,18 +687,21 @@
             made[0, q] = (tin[row_block(0, j, q)].astype(F32) + totals[q]).astype(BF16)
         to_partner_segment(made.at[0])
         from_partner_segment()
-        scatter_hidden_grads(pin, lambda: exchange(rows_back, 1))
+        scatter_hidden_grads(pin, lambda: None)
         write_hidden_grads()
         gather_hidden_grads(lambda: None)
+        pl.semaphore_signal(go_sem, inc=1, device_id=partner, device_id_type=MESH)
         tensor_send(1)
-        exchanged(rows_back, 1)
-        back = send(rows_back, rows_back, fwd_sem.at[0, 1], fwd_sem.at[1, 1], partner)
+        exchange(rows_back, 1)
         totals = tensor_sum(1)
         for q in range(per):
             made[1, q] = totals[q].astype(BF16)
         to_rows(made.at[1], rows_last)
+        exchanged(rows_back, 1)
+        back = send(rows_back, rows_back, fwd_sem.at[0, 1], fwd_sem.at[1, 1], partner)
         arrived(rows_early, fwd_sem.at[1, 0])
-        put_rows(acts, rows_early)
+        put_rows(out_early, rows_early)
+        put_rows(out_back, rows_back)
         rows_arrived(rows_last)
         factor = inv[:, 0:1]
         project = jnp.zeros((rows, width), F32)
@@ -711,7 +712,7 @@
         for b in range(dp_count):
             weighted = rows_last[b].astype(F32) * gain_all[b : b + 1, :]
             unit = blocks[b].astype(F32) * factor
-            grads[0, :, b * width : (b + 1) * width] = (rows_back[b].astype(F32) + factor * (weighted - unit * mean)).astype(BF16)
+            out_last[0, :, b * width : (b + 1) * width] = (rows_back[b].astype(F32) + factor * (weighted - unit * mean)).astype(BF16)
         back.wait_send()
         drain_exchange(rows_back, 1)
 
@@ -756,12 +757,14 @@
         totals = tensor_sum(1)
         for q in range(per):
             made[1, q] = (pin[row_block(1, j, q)].astype(F32) + totals[q]).astype(BF16)
+        pl.semaphore_wait(go_sem, 1)
         to_rows(made.at[1], rows_last)
         ahead = send(rows_early, rows_early, fwd_sem.at[0, 0], fwd_sem.at[1, 0], partner)
         arrived(rows_back, fwd_sem.at[1, 1])
-        put_rows(grads, rows_back)
+        put_rows(out_early, rows_early)
+        put_rows(out_back, rows_back)
         rows_arrived(rows_last)
-        put_rows(acts, rows_last)
+        put_rows(out_last, rows_last)
         ahead.wait_send()
         drain_exchange(rows_early, 0)
         arrived(st_in.at[pl.ds(1, dp_count - 1)], st_sem.at[0])
@@ -836,7 +839,7 @@
             dma((5 + Z,)),
             dma((2, 4, 2, 2)),
             dma((5 + Z,)),
-            dma((2, 3, 4, 2)),
+            dma((2, 3, 4, 2, 2)),
             dma((2, 6)),
             dma((2, 2)),
             dma((2,)),
@@ -847,16 +850,17 @@
         ]
         vmem = pl.BlockSpec(memory_space=pltpu.VMEM)
         hbm = pl.BlockSpec(memory_space=pl.ANY)
-        acts, grads = pl.pallas_call(
+        early_rows, last_rows, back_rows = pl.pallas_call(
             functools.partial(kernel, (dp_count, tensor_count, rows, width, hidden)),
-            out_shape=[jax.ShapeDtypeStruct((1, rows, model), BF16)] * 2,
+            out_shape=[jax.ShapeDtypeStruct((1, rows, model), BF16)] * 3,
             in_specs=[hbm, hbm, vmem, hbm, hbm, hbm],
-            out_specs=[vmem, vmem],
+            out_specs=[vmem, vmem, vmem],
             scratch_shapes=scratch,
             compiler_params=pltpu.CompilerParams(collective_id=0, has_side_effects=True),
         )(tokens, cotangent, gains, w_gate, w_up, w_down)
 
-        return acts, grads
+        lead = lax.axis_index("segment") == 0
+        return jnp.where(lead, early_rows, last_rows), jnp.where(lead, last_rows, back_rows)
 
     in_specs = (
         P("dp", None),

time: 193 us -> 190 us (0.984)
  local copies, waits for them, and re-layouts: 3.18 us -> 0 us
  Pallas kernels: 188 us -> 186 us
    unnamed x2 -> x0, local copies, waits for them, and re-layouts: 3.18 us -> none
    pallas_call x1, Pallas kernels: 188 us -> 186 us  [body(): pl.pallas_call(functools.partial(kernel, (dp_count, tensor_count, rows, w...]
where the time goes in v4:
time: 190 us; the launch traced here: 188 us
  Pallas kernels  186 us (98%)
    pallas_call x1, Pallas kernels, body(): pl.pallas_call(functools.partial(kernel, (dp_count, tensor_count, rows, w...  186 us

profile of v4, /device:TPU:8, one launch (start us, length us, event | category | flops | bytes accessed | tf_op | source)
XLA Modules:
  0.0 188.3 jit_solution(4148982321755485997)
XLA Ops:
  0.6 185.9 %shard_map.77 = (bf16[1,16,5120]{2,1,0:T(8,128)(2,1)}, bf16[1,16,5120]{2,1,0:T(8,128)(2,1)}, bf16[1,16,5120]{2,1,0:T(8,128)(2,1)}) custom-call(bf16[16,5120]{1,0:T(8,128)(2,1)} %tokens_hbm.1, bf16[16,5120]{1,0:T(8,128)(2,1)} %cotangent_hbm.1, f32[1,5120]{1,0:T(1,128)} %gains.1, bf16[1,320,3456]{2,1,0:T(8,128)(2,1)} %wg_hbm.1, bf16[1,320,3456]{2,1,0:T(8,128)(2,1)} %wu_hbm.1, ...), custom_call_target="tpu_custom_call" | custom-call | tf_op jit(solution)/shard_map/pallas_call | solution.py:853
  186.5 1.8 broadcast_select_fusion

commit v5 on v4

--- a/solution.py
+++ b/solution.py
@@ -106,6 +106,8 @@
         return (seg, y * Z + lax.rem(m + (Z - steps if d == 0 else steps), Z), j)
 
     others = pl.ds(0, dp_count - 1)
+    dp_far = sorted(range(1, dp_count), key=lambda r: -min(r % Z, Z - r % Z))
+    tensor_far = sorted(range(1, tensor_count), key=lambda r: (r % 2 == 0, -min(r, tensor_count - r)))
 
     def at(offset):
         return lax.rem(m + offset + Z, Z)
@@ -132,7 +134,7 @@
         pltpu.make_async_copy(ref, ref, sem).wait()
 
     barrier = pltpu.get_barrier_semaphore()
-    for r in range(1, dp_count):
+    for r in dp_far:
         pl.semaphore_signal(barrier, inc=1, device_id=dp_peer(r), device_id_type=MESH)
     for r in range(1, tensor_count):
         pl.semaphore_signal(barrier, inc=1, device_id=(seg, i, tensor_at(r)), device_id_type=MESH)
@@ -170,7 +172,7 @@
     def _():
         pl.semaphore_wait(go_sem, 1)
 
-    for r in range(1, dp_count):
+    for r in dp_far:
         to = lax.rem(i + r, dp_count)
         send(blocks.at[to], tin.at[i], in_sem.at[0], in_sem.at[1], (seg, to, j))
 
@@ -493,7 +495,7 @@
 
     def tensor_send(turn):
         t_out[turn] = acc[...].reshape(dp_count, rows, width).astype(BF16)
-        for r in range(1, tensor_count):
+        for r in tensor_far:
             jd = tensor_at(r)
             for q in range(per):
                 send(
@@ -514,7 +516,7 @@
         return totals
 
     def to_partner_segment(src):
-        for r in range(tensor_count):
+        for r in (*tensor_far, 0):
             send(src, pin.at[pl.ds(per * j, per)], p_sem.at[0], p_sem.at[1], (1 - seg, i, tensor_at(r)))
 
     @jax.named_scope("wait_seg")
@@ -524,7 +526,7 @@
     @jax.named_scope("exchange")
     def exchange(land, kind):
         land[i] = pin[i]
-        for r in range(1, dp_count):
+        for r in dp_far:
             send(pin.at[lax.rem(i + r, dp_count)], land.at[i], row_sem.at[kind, 0], row_sem.at[kind, 1], dp_peer(r))
 
     @jax.named_scope("exchanged")
@@ -536,7 +538,7 @@
 
     @jax.named_scope("to_rows")
     def to_rows(src, land):
-        for r in range(tensor_count):
+        for r in (*tensor_far, 0):
             for q in range(per):
                 to = (seg, row_block(1, j, q), tensor_at(r))
                 out, into = row_sem.at[2, 0], row_sem.at[2, 1]
@@ -736,7 +738,7 @@
             preferred_element_type=F32,
             precision=lax.Precision.HIGHEST,
         )
-        for r in range(1, dp_count):
+        for r in dp_far:
             send(st_out, st_in.at[r], st_sem.at[0], st_sem.at[1], dp_peer(r))
         advance(steps, 2)
         with jax.named_scope("st"):

time: 190 us -> 186 us (0.979)
  Pallas kernels: 186 us -> 183 us
    pallas_call x1, Pallas kernels: 186 us -> 183 us  [body(): pl.pallas_call(functools.partial(kernel, (dp_count, tensor_count, rows, w...]
where the time goes in v5:
time: 186 us; the launch traced here: 185 us
  Pallas kernels  183 us (98%)
    pallas_call x1, Pallas kernels, body(): pl.pallas_call(functools.partial(kernel, (dp_count, tensor_count, rows, w...  183 us

profile of v5, /device:TPU:8, one launch (start us, length us, event | category | flops | bytes accessed | tf_op | source)
XLA Modules:
  0.0 185.4 jit_solution(17440082179628271013)
XLA Ops:
  0.6 183.0 %shard_map.77 = (bf16[1,16,5120]{2,1,0:T(8,128)(2,1)}, bf16[1,16,5120]{2,1,0:T(8,128)(2,1)}, bf16[1,16,5120]{2,1,0:T(8,128)(2,1)}) custom-call(bf16[16,5120]{1,0:T(8,128)(2,1)} %tokens_hbm.1, bf16[16,5120]{1,0:T(8,128)(2,1)} %cotangent_hbm.1, f32[1,5120]{1,0:T(1,128)} %gains.1, bf16[1,320,3456]{2,1,0:T(8,128)(2,1)} %wg_hbm.1, bf16[1,320,3456]{2,1,0:T(8,128)(2,1)} %wu_hbm.1, ...), custom_call_target="tpu_custom_call" | custom-call | tf_op jit(solution)/shard_map/pallas_call | solution.py:855
  183.6 1.8 broadcast_select_fusion

commit v6 on v5

--- a/solution.py
+++ b/solution.py
@@ -591,15 +591,11 @@
         pl.semaphore_wait(go_sem, 1)
         scatter_hidden_grads(tin, lambda: None)
         from_partner_segment()
+        exchange(rows_early, 0)
         scale(pin)
 
     loads[0].wait()
     loads[1].wait()
-
-    def hand_early_rows():
-        @pl.when(late)
-        def _():
-            exchange(rows_early, 0)
 
     def drain_exchange(land, kind):
         arrived(land.at[others], row_sem.at[kind, 0])
@@ -609,7 +605,7 @@
             pg, 0, hidden, pu, 0, hidden, gu_y, gu_ring_y, gu_ring_z, gu_out, gu_fin, gu_sem, gu_ysem,
             lambda c, w: spread(xg[...], wg, pg, c, w),
             lambda c, w: spread(xg[...], wu, pu, c, w),
-            hand_early_rows,
+            lambda: None,
             GU_FAR,
         )
 

time: 186 us -> 185 us (level)
  no operation moved by 1% of the time
where the time goes in v6:
time: 185 us
  Pallas kernels  182 us (98%)
    pallas_call x1, Pallas kernels, body(): pl.pallas_call(functools.partial(kernel, (dp_count, tensor_count, rows, w...  182 us

profile of v6, /device:TPU:8, one launch (start us, length us, event | category | flops | bytes accessed | tf_op | source)
XLA Modules:
  0.0 184.7 jit_solution(7324770174700291484)
XLA Ops:
  0.6 182.3 %shard_map.77 = (bf16[1,16,5120]{2,1,0:T(8,128)(2,1)}, bf16[1,16,5120]{2,1,0:T(8,128)(2,1)}, bf16[1,16,5120]{2,1,0:T(8,128)(2,1)}) custom-call(bf16[16,5120]{1,0:T(8,128)(2,1)} %tokens_hbm.1, bf16[16,5120]{1,0:T(8,128)(2,1)} %cotangent_hbm.1, f32[1,5120]{1,0:T(1,128)} %gains.1, bf16[1,320,3456]{2,1,0:T(8,128)(2,1)} %wg_hbm.1, bf16[1,320,3456]{2,1,0:T(8,128)(2,1)} %wu_hbm.1, ...), custom_call_target="tpu_custom_call" | custom-call | tf_op jit(solution)/shard_map/pallas_call | solution.py:851
  183.0 1.8 broadcast_select_fusion
